TPU v7x, 256 devices: a whole 4x4x8 slice. The times are simulated.
256 devices in a mesh: pipe: 4 (over y), tensor: 32 (over x, z_hi, core), dp: 2 (over z_lo).
Axes of the slice: x: 4, y: 4, z: 8 (z_hi: 4, z_lo: 2; z = z_hi * 2 + z_lo), core: 2. Of those that a mesh axis runs over, the one named last changes fastest.
Arguments:
- weight_main: bfloat16 [4, 4096, 2, 8192], P('pipe', None, None, 'tensor'), may hold values from -0.09375 to 0.09375
- weight_state: bfloat16 [4, 4096, 2, 1024], P('pipe', None, None, 'tensor'), may hold values from -0.09375 to 0.09375
- weight_step: bfloat16 [4, 128, 4096], P('pipe', 'tensor'), may hold values from -0.09375 to 0.09375
- weight_out: bfloat16 [4, 8192, 4096], P('pipe', 'tensor'), may hold values from -0.0625 to 0.0625
- conv_main: float32 [4, 4, 8192], P('pipe', None, 'tensor'), may hold values from -3 to 3
- conv_state: float32 [4, 4, 2, 1024], P('pipe'), may hold values from -3 to 3
- step_bias: float32 [4, 128], P('pipe', 'tensor'), may hold values from -3 to 0
- decay_log: float32 [4, 128], P('pipe', 'tensor'), may hold values from -5 to 0.5
- skip_gain: float32 [4, 128], P('pipe', 'tensor'), may hold values from 1 to 6
- norm_gain: float32 [4, 8192], P('pipe', 'tensor'), may hold values from 0.5 to 1.5
- saved_main: bfloat16 [4, 256, 2, 8192], P('pipe', 'dp', None, 'tensor'), parts along dimension 1, may hold values from -6 to 6
- saved_state: bfloat16 [4, 256, 2, 1024], P('pipe', 'dp'), parts along dimension 1, may hold values from -6 to 6
- saved_step: bfloat16 [4, 128, 256], P('pipe', 'tensor', 'dp'), parts along dimension 2, may hold values from -6 to 6
- output_grad: bfloat16 [256, 4096], P('dp', 'tensor'), parts along dimension 0, may hold values from -6 to 6
Outputs:
- input_grads: bfloat16 [4, 256, 4096], P('pipe', 'dp', 'tensor'), parts along dimension 1
There are 2 independent parts, one for each index of `dp`. A program takes and returns all parts, laid end to end along the dimension named above; an argument that names none is the same for every part. Nothing has to cross between parts.
All inputs are finite; a program needn't handle non-finite values.
Results may differ from a plain program's by a relative error of at most 0.02.
Values may be sent and summed in bfloat16 or wider, within the bound.
A program may use at most 64 MiB of HBM per device.

v0:
```python
import jax
import jax.numpy as jnp
from jax import lax
from jax.sharding import PartitionSpec as P

NSTATE = 128
GROUP_SPAN = 4
STRETCH = 128


EPSILON = 1e-05
HIGHEST = lax.Precision.HIGHEST


def from_partner(value, axis, bit):
    mask = 2**bit
    pairs = [(source, source ^ mask) for source in range(lax.axis_size(axis))]
    return lax.ppermute(value, axis, pairs)


def passed_along(value, axis, steps):
    count = lax.axis_size(axis)
    leading, last = (max(0, -steps), min(count, count - steps))
    return lax.ppermute(value, axis, [(source, source + steps) for source in range(leading, last)])


def causal_conv(signal, kernel):
    taps = kernel.shape[0]
    length = signal.shape[0]
    padded = jnp.pad(signal, ((taps - 1, 0), (0, 0)))
    summed = kernel[0] * padded[0:length]
    for offset in range(1, taps):
        summed = summed + kernel[offset] * padded[offset : offset + length]
    return summed


def state_space(values, step_sizes, decay_rates, inputs, readout):
    length, head_count, head_size = values.shape
    blocks = length // STRETCH
    state_width = inputs.shape[1]
    decays = (step_sizes * decay_rates[:, None]).reshape(head_count, blocks, STRETCH)
    running = jnp.cumsum(decays, axis=2)
    scaled = (values * step_sizes.T[:, :, None]).reshape(blocks, STRETCH, head_count, head_size)
    inputs_blocked = inputs.reshape(blocks, STRETCH, state_width)
    readout_blocked = readout.reshape(blocks, STRETCH, state_width)
    scores = jnp.einsum("cin,cjn->cij", readout_blocked, inputs_blocked, precision=HIGHEST)
    position = jnp.arange(STRETCH)
    causal = position[:, None] >= position[None, :]
    differ = running[:, :, :, None] - running[:, :, None, :]
    weights = jnp.where(causal, jnp.exp(jnp.where(causal, differ, 0.0)), 0.0) * scores[None]
    within = jnp.einsum("hcij,cjhp->cihp", weights, scaled, precision=HIGHEST)
    tail_decay = jnp.exp(running[:, :, -1:] - running)
    weighted = scaled * jnp.transpose(tail_decay, (1, 2, 0))[:, :, :, None]
    block_sums = jnp.einsum("cjhp,cjn->chpn", weighted, inputs_blocked, precision=HIGHEST)
    shrinks = jnp.exp(running[:, :, -1]).T

    def advance(carried, item):
        newest, shrink = item
        return (carried * shrink[:, None, None] + newest, carried)

    anchor = jnp.zeros((head_count, head_size, state_width), jnp.float32)
    _, entering = lax.scan(advance, anchor, (block_sums, shrinks))
    across = jnp.einsum("cin,chpn->cihp", readout_blocked, entering, precision=HIGHEST)
    across = across * jnp.transpose(jnp.exp(running), (1, 2, 0))[:, :, :, None]
    return (within + across).reshape(length, head_count, head_size)


def mamba_mixer(
    main_proj,
    state_proj,
    step_proj,
    conv_main,
    conv_state,
    step_bias,
    decay_log,
    skip_gain,
    norm_gain,
):
    length = main_proj.shape[0]
    head_count = step_proj.shape[0]
    gating = main_proj[:, 0]
    mixed_in = jax.nn.silu(causal_conv(main_proj[:, 1], conv_main))
    flat_state = state_proj.reshape(length, -1)
    state_conv = jax.nn.silu(
        causal_conv(flat_state, conv_state.reshape(conv_state.shape[0], -1))
    ).reshape(length, 2, -1)
    step_sizes = jax.nn.softplus(step_proj + step_bias[:, None])
    decay_rates = -jnp.exp(decay_log)
    values = mixed_in.reshape(length, head_count, -1)
    scanned = state_space(values, step_sizes, decay_rates, state_conv[:, 0], state_conv[:, 1])
    scanned = scanned + skip_gain[None, :, None] * values
    gated = scanned.reshape(length, -1) * jax.nn.silu(gating)
    inverse = lax.rsqrt(jnp.mean(gated * gated, axis=1, keepdims=True) + EPSILON)
    return gated * inverse * norm_gain


def body(
    weight_main,
    weight_state,
    weight_step,
    weight_out,
    conv_main,
    conv_state,
    step_bias,
    decay_log,
    skip_gain,
    norm_gain,
    saved_main,
    saved_state,
    saved_step,
    output_grad,
):
    sections = lax.axis_size("pipe")
    section = lax.axis_index("pipe")
    tensor_index = lax.axis_index("tensor")
    member = tensor_index % GROUP_SPAN
    group = tensor_index // GROUP_SPAN
    span_bits = GROUP_SPAN.bit_length() - 1
    length = saved_main.shape[1]
    col_count = output_grad.shape[1]
    model_width = weight_out.shape[2]
    main_cols = weight_main[0].reshape(model_width, -1)
    state_cols = weight_state[0].reshape(model_width, -1)
    step_rows = weight_step[0]
    out_rows = weight_out[0]
    state_group = lax.dynamic_slice_in_dim(saved_state[0], group * NSTATE, NSTATE, 2)
    conv_group = lax.dynamic_slice_in_dim(conv_state[0], group * NSTATE, NSTATE, 2)

    def local_mixer(first_in, second_in, third_in):
        return mamba_mixer(
            first_in,
            second_in,
            third_in,
            conv_main[0],
            conv_group,
            step_bias[0],
            decay_log[0],
            skip_gain[0],
            norm_gain[0],
        )

    _, pullback = jax.vjp(
        local_mixer,
        saved_main[0].astype(jnp.float32),
        state_group.astype(jnp.float32),
        saved_step[0].astype(jnp.float32),
    )
    result = jnp.zeros((length, col_count), jnp.bfloat16)
    incoming = output_grad
    for moment in range(sections):
        back_grad_main, back_grad_state, back_grad_step = pullback(
            lax.dot_general(
                lax.all_gather(incoming, "tensor", axis=1, tiled=True),
                out_rows,
                (((1,), (1,)), ((), ())),
                preferred_element_type=jnp.float32,
            )
        )
        kept = back_grad_state
        for bit in range(span_bits - 1, -1, -1):
            half = kept.shape[2] // 2
            lower = kept[:, :, :half]
            upper = kept[:, :, half:]
            high = member // 2**bit % 2 == 1
            own = jnp.where(high, upper, lower)
            other = jnp.where(high, lower, upper)
            kept = own + from_partner(other, "tensor", bit)
        grad_main = back_grad_main.astype(jnp.bfloat16).reshape(length, -1)
        grad_state = kept.astype(jnp.bfloat16).reshape(length, -1)
        grad_step = back_grad_step.astype(jnp.bfloat16)
        summed = lax.dot_general(
            main_cols, grad_main, (((1,), (1,)), ((), ())), preferred_element_type=jnp.float32
        )
        summed = summed + lax.dot_general(
            state_cols, grad_state, (((1,), (1,)), ((), ())), preferred_element_type=jnp.float32
        )
        owned = lax.psum_scatter(
            summed
            + lax.dot_general(
                step_rows, grad_step, (((0,), (0,)), ((), ())), preferred_element_type=jnp.float32
            ),
            "tensor",
            scatter_dimension=0,
            tiled=True,
        ).T.astype(jnp.bfloat16)
        result = jnp.where(section == sections - 1 - moment, owned, result)
        if moment + 1 < sections:
            incoming = passed_along(owned, "pipe", -1)
    return result[None]


def solution(mesh):
    return jax.shard_map(
        body,
        mesh=mesh,
        in_specs=(
            P("pipe", None, None, "tensor"),
            P("pipe", None, None, "tensor"),
            P("pipe", "tensor", None),
            P("pipe", "tensor", None),
            P("pipe", None, "tensor"),
            P("pipe", None, None, None),
            P("pipe", "tensor"),
            P("pipe", "tensor"),
            P("pipe", "tensor"),
            P("pipe", "tensor"),
            P("pipe", "dp", None, "tensor"),
            P("pipe", "dp", None, None),
            P("pipe", "tensor", "dp"),
            P("dp", "tensor"),
        ),
        out_specs=P("pipe", "dp", "tensor"),
        check_vma=False,
    )
```

profile of v0, /device:TPU:1, one launch (start us, length us, event | category | flops | bytes accessed | tf_op | source)
XLA Modules:
  0.0 772.3 jit_solution(89910686781437993)
XLA Ops:
  20.5 4.9 copy.113
  25.4 40.8 %all-gather.5.cloned.1.call-done = bf16[128,4096]{1,0:T(8,128)(2,1)} async-done(((bf16[128,128]{1,0:T(8,128)(2,1)}), bf16[128,4096]{1,0:T(8,128)(2,1)}) %all-gather.5.cloned.1.call-update) | async-done | bytes 1048592 | tf_op jit(solution)/shard_map/all_gather | solution.py:153
  66.2 2.1 multiply_reduce_fusion.13
  70.5 2.3 fusion.49
  73.4 2.8 fusion.63
  76.2 1.7 copy.58
  77.9 1.8 broadcast_multiply_fusion.31
  89.5 1.7 copy.60
  91.3 5.2 fusion.193
  99.8 2.5 reduce_window_sum.50
  103.2 2.0 convolution_add_fusion.7
  105.3 1.9 fusion.3
  107.3 87.1 %reduce-scatter.5.cloned.1.call-done = f32[128,128]{0,1:T(8,128)} async-done(((f32[4096,128]{0,1:T(8,128)}), f32[128,128]{0,1:T(8,128)}) %reduce-scatter.5.cloned.1.call-update) | async-done | bytes 65552 | tf_op jit(solution)/shard_map/reduce_scatter | solution.py:177
  195.3 1.3 collective-permute-start.2
  196.6 3.5 collective-permute-done.2
  200.3 53.1 %all-gather.7.cloned.1.call-done = bf16[128,4096]{1,0:T(8,128)(2,1)} async-done(((bf16[128,128]{1,0:T(8,128)(2,1)}), bf16[128,4096]{1,0:T(8,128)(2,1)}) %all-gather.7.cloned.1.call-update) | async-done | bytes 1048592 | tf_op jit(solution)/shard_map/all_gather | solution.py:153
  253.5 2.2 multiply_reduce_fusion.9
  256.2 1.6 fusion.185
  257.8 1.6 copy.72
  259.5 2.3 fusion.51
  261.8 2.8 fusion.62
  265.2 1.7 copy.77
  271.0 1.7 copy.103
  275.0 1.7 copy.107
  276.7 1.5 slice_select_fusion.2
  279.0 1.7 copy.73
  282.5 1.6 add_convert_fusion.2
  284.1 1.7 copy.75
  285.8 5.2 fusion.194
  294.3 2.5 reduce_window_sum.52
  297.7 2.0 convolution_add_fusion.5
  299.9 1.9 fusion.2
  301.9 87.4 %reduce-scatter.7.cloned.1.call-done = f32[128,128]{0,1:T(8,128)} async-done(((f32[4096,128]{0,1:T(8,128)}), f32[128,128]{0,1:T(8,128)}) %reduce-scatter.7.cloned.1.call-update) | async-done | bytes 65552 | tf_op jit(solution)/shard_map/reduce_scatter | solution.py:177
  390.1 1.3 collective-permute-start.5
  391.4 3.5 collective-permute-done.5
  394.9 53.4 %all-gather.9.cloned.1.call-done = bf16[128,4096]{1,0:T(8,128)(2,1)} async-done(((bf16[128,128]{1,0:T(8,128)(2,1)}), bf16[128,4096]{1,0:T(8,128)(2,1)}) %all-gather.9.cloned.1.call-update) | async-done | bytes 1048592 | tf_op jit(solution)/shard_map/all_gather | solution.py:153
  448.3 2.2 multiply_reduce_fusion.7
  451.1 1.6 fusion.183
  452.6 1.6 copy.82
  454.3 2.3 fusion.53
  456.6 2.8 fusion.61
  460.0 1.7 copy.87
  465.8 1.7 copy.104
  469.8 1.7 copy.108
  471.5 1.5 slice_select_fusion.1
  473.8 1.7 copy.83
  477.3 1.6 add_convert_fusion.1
  478.9 1.7 copy.85
  480.6 5.2 fusion.195
  489.1 2.5 reduce_window_sum.54
  492.5 2.0 convolution_add_fusion.3
  494.6 1.9 fusion.1
  496.6 87.3 %reduce-scatter.9.cloned.1.call-done = f32[128,128]{0,1:T(8,128)} async-done(((f32[4096,128]{0,1:T(8,128)}), f32[128,128]{0,1:T(8,128)}) %reduce-scatter.9.cloned.1.call-update) | async-done | bytes 65552 | tf_op jit(solution)/shard_map/reduce_scatter | solution.py:177
  586.1 3.5 collective-permute-done.8
  589.6 53.4 %all-gather.11.cloned.1.call-done = bf16[128,4096]{1,0:T(8,128)(2,1)} async-done(((bf16[128,128]{1,0:T(8,128)(2,1)}), bf16[128,4096]{1,0:T(8,128)(2,1)}) %all-gather.11.cloned.1.call-update) | async-done | bytes 1048592 | tf_op jit(solution)/shard_map/all_gather | solution.py:153
  643.0 2.2 multiply_reduce_fusion.5
  645.7 1.6 fusion.181
  648.3 2.3 fusion.55
  650.6 2.7 fusion.60
  664.4 5.1 fusion.196
  672.4 2.1 convolution_add_fusion.1
  674.5 1.9 fusion
  676.5 87.5 %reduce-scatter.11.cloned.1.call-done = f32[128,128]{0,1:T(8,128)} async-done(((f32[4096,128]{0,1:T(8,128)}), f32[128,128]{0,1:T(8,128)}) %reduce-scatter.11.cloned.1.call-update) | async-done | bytes 65552 | tf_op jit(solution)/shard_map/reduce_scatter | solution.py:177
  764.0 1.5 fusion.120
  (327 shorter events, 79.0 us)
Async XLA Ops:
  6.5 59.7 %copy-start = (bf16[1,256,4096]{2,1,0:T(8,128)(2,1)S(1)}, bf16[1,256,4096]{2,1,0:T(8,128)(2,1)}, u32[]{:S(2)}) copy-start(bf16[1,256,4096]{2,1,0:T(8,128)(2,1)} %param.17) | copy-start | bytes 6291460
  6.5 4.8 copy-start.86
  6.5 4.8 copy-start.54
  6.5 4.8 copy-start.45
  6.5 59.7 %all-gather.5.cloned.1.call-start = ((), (), s32[]{:S(2)}) async-start(), calls=%async_computation.4 | async-start | bytes 1081344 | tf_op jit(solution)/shard_map/all_gather | solution.py:153
  7.3 187.2 %reduce-scatter.5.cloned.1.call-start = ((), (), s32[]{:S(2)}) async-start(), calls=%async_computation.5 | async-start | bytes 2162688 | tf_op jit(solution)/shard_map/reduce_scatter | solution.py:177
  8.3 8.3 %copy-start.85 = (f32[1,4]{1,0:T(1,128)S(1)}, f32[1,4]{1,0:T(1,128)}, u32[]{:S(2)}) copy-start(f32[1,4]{1,0:T(1,128)} %param.22) | copy-start | bytes 52
  10.1 7.3 copy-start.50
  11.1 57.8 %copy-start.2 = (f32[128,2,256]{2,0,1:T(8,128)}, f32[128,2,256]{2,0,1:T(8,128)S(1)}, u32[]{:S(2)}) copy-start(f32[128,2,256]{2,0,1:T(8,128)S(1)} %bitcast_convert_fusion) | copy-start | bytes 786436
  11.3 14.1 %copy-start.31 = (f32[128,256]{0,1:T(8,128)}, f32[128,256]{0,1:T(8,128)S(1)}, u32[]{:S(2)}) copy-start(f32[128,256]{0,1:T(8,128)S(1)} %copy.52) | copy-start | bytes 393220
  12.7 3.8 copy-start.63
  12.8 3.7 copy-start.60
  68.3 11.3 %copy-start.6 = (f32[128,256]{1,0:T(8,128)}, f32[128,256]{1,0:T(8,128)S(1)}, u32[]{:S(2)}) copy-start(f32[128,256]{1,0:T(8,128)S(1)} %get-tuple-element.152) | copy-start | bytes 393220
  69.7 11.2 %copy-start.25 = (f32[128,256]{1,0:T(8,128)S(1)}, f32[128,256]{1,0:T(8,128)}, u32[]{:S(2)}) copy-start(f32[128,256]{1,0:T(8,128)} %get-tuple-element.145) | copy-start | bytes 393220
  79.7 7.3 copy-start.40
  79.7 7.3 copy-start.42
  79.7 7.3 copy-start.44
  81.0 7.0 copy-start.10
  82.5 6.4 copy-start.24
  85.4 5.8 copy-start.14
  86.1 10.4 %collective-permute-start = (f32[128,2,64]{0,2,1:T(8,128)}, f32[128,2,64]{0,2,1:T(8,128)}, u32[]{:S(2)}, u32[]{:S(2)}) collective-permute-start(f32[128,2,64]{0,2,1:T(8,128)} %slice_select_fusion.3), channel_id=1, source_target_pairs={{0,4},{2,6},{4,0},{6,2},{8,12},{10,14},{12,8},{14,10},{16,20},{18,... | collective-permute-start | bytes 196616 | tf_op jit(solution)/shard_map/ppermute | solution.py:18
  91.2 5.2 copy-start.28
  91.2 5.3 copy-start.15
  91.2 7.9 %copy-start.59 = (f32[4,1,128]{2,1,0:T(1,128)S(1)}, f32[4,1,128]{2,1,0:T(1,128)}, u32[]{:S(2)}) copy-start(f32[4,1,128]{2,1,0:T(1,128)} %get-tuple-element.142) | copy-start | bytes 6148
  91.2 7.9 %copy-start.62 = (f32[128,4]{0,1:T(4,128)S(1)}, f32[128,4]{0,1:T(4,128)}, u32[]{:S(2)}) copy-start(f32[128,4]{0,1:T(4,128)} %copy-done.61) | copy-start | bytes 6148
  91.2 7.9 %copy-start.73 = (f32[4,128]{1,0:T(4,128)S(1)}, f32[4,128]{1,0:T(4,128)}, u32[]{:S(2)}) copy-start(f32[4,128]{1,0:T(4,128)} %neg.67) | copy-start | bytes 6148
  91.2 7.9 %copy-start.81 = (f32[4,128]{1,0:T(4,128)S(1)}, f32[4,128]{1,0:T(4,128)}, u32[]{:S(2)}) copy-start(f32[4,128]{1,0:T(4,128)} %get-tuple-element.84) | copy-start | bytes 6148
  91.3 11.9 %copy-start.1 = (bf16[1,4096,2,32]{1,3,2,0:T(8,128)(2,1)S(1)}, bf16[1,4096,2,32]{1,3,2,0:T(8,128)(2,1)}, u32[]{:S(2)}) copy-start(bf16[1,4096,2,32]{1,3,2,0:T(8,128)(2,1)} %param.15) | copy-start | bytes 1572868
  98.6 3.7 collective-permute-start.1
  107.3 146.2 %all-gather.7.cloned.1.call-start = ((), (), s32[]{:S(2)}) async-start(), calls=%async_computation.6 | async-start | bytes 1081344 | tf_op jit(solution)/shard_map/all_gather | solution.py:153
  195.3 4.8 collective-permute-start.2
  200.1 189.2 %reduce-scatter.7.cloned.1.call-start = ((), (), s32[]{:S(2)}) async-start(), calls=%async_computation.7 | async-start | bytes 2162688 | tf_op jit(solution)/shard_map/reduce_scatter | solution.py:177
  278.2 12.8 %collective-permute-start.3 = (f32[128,2,64]{0,2,1:T(8,128)}, f32[128,2,64]{0,2,1:T(8,128)}, u32[]{:S(2)}, u32[]{:S(2)}) collective-permute-start(f32[128,2,64]{0,2,1:T(8,128)} %slice_select_fusion.2), channel_id=1, source_target_pairs={{0,4},{2,6},{4,0},{6,2},{8,12},{10,14},{12,8},{14,10},{16,20},{18,... | collective-permute-start | bytes 196616 | tf_op jit(solution)/shard_map/ppermute | solution.py:18
  285.8 5.2 copy-start.29
  285.8 5.2 copy-start.12
  285.8 7.9 %copy-start.51 = (f32[4,1,128]{2,1,0:T(1,128)S(1)}, f32[4,1,128]{2,1,0:T(1,128)}, u32[]{:S(2)}) copy-start(f32[4,1,128]{2,1,0:T(1,128)} %get-tuple-element.140) | copy-start | bytes 6148
  285.8 7.9 %copy-start.75 = (f32[4,128]{1,0:T(4,128)S(1)}, f32[4,128]{1,0:T(4,128)}, u32[]{:S(2)}) copy-start(f32[4,128]{1,0:T(4,128)} %neg.69) | copy-start | bytes 6148
  285.8 7.9 %copy-start.83 = (f32[4,128]{1,0:T(4,128)S(1)}, f32[4,128]{1,0:T(4,128)}, u32[]{:S(2)}) copy-start(f32[4,128]{1,0:T(4,128)} %get-tuple-element.82) | copy-start | bytes 6148
  293.1 3.8 collective-permute-start.4
  301.8 146.5 %all-gather.9.cloned.1.call-start = ((), (), s32[]{:S(2)}) async-start(), calls=%async_computation.8 | async-start | bytes 1081344 | tf_op jit(solution)/shard_map/all_gather | solution.py:153
  390.1 4.8 collective-permute-start.5
  394.9 189.1 %reduce-scatter.9.cloned.1.call-start = ((), (), s32[]{:S(2)}) async-start(), calls=%async_computation.9 | async-start | bytes 2162688 | tf_op jit(solution)/shard_map/reduce_scatter | solution.py:177
  448.3 2.8 copy-start.8
  473.0 12.8 %collective-permute-start.6 = (f32[128,2,64]{0,2,1:T(8,128)}, f32[128,2,64]{0,2,1:T(8,128)}, u32[]{:S(2)}, u32[]{:S(2)}) collective-permute-start(f32[128,2,64]{0,2,1:T(8,128)} %slice_select_fusion.1), channel_id=1, source_target_pairs={{0,4},{2,6},{4,0},{6,2},{8,12},{10,14},{12,8},{14,10},{16,20},{18,... | collective-permute-start | bytes 196616 | tf_op jit(solution)/shard_map/ppermute | solution.py:18
  480.6 5.2 copy-start.30
  480.6 5.2 copy-start.13
  480.6 7.9 %copy-start.52 = (f32[4,1,128]{2,1,0:T(1,128)S(1)}, f32[4,1,128]{2,1,0:T(1,128)}, u32[]{:S(2)}) copy-start(f32[4,1,128]{2,1,0:T(1,128)} %get-tuple-element.140) | copy-start | bytes 6148
  480.6 7.9 %copy-start.76 = (f32[4,128]{1,0:T(4,128)S(1)}, f32[4,128]{1,0:T(4,128)}, u32[]{:S(2)}) copy-start(f32[4,128]{1,0:T(4,128)} %neg.71) | copy-start | bytes 6148
  480.6 7.9 %copy-start.84 = (f32[4,128]{1,0:T(4,128)S(1)}, f32[4,128]{1,0:T(4,128)}, u32[]{:S(2)}) copy-start(f32[4,128]{1,0:T(4,128)} %get-tuple-element.80) | copy-start | bytes 6148
  487.9 3.7 collective-permute-start.7
  496.6 146.4 %all-gather.11.cloned.1.call-start = ((), (), s32[]{:S(2)}) async-start(), calls=%async_computation.10 | async-start | bytes 1081344 | tf_op jit(solution)/shard_map/all_gather | solution.py:153
  584.8 4.8 collective-permute-start.8
  589.6 174.4 %reduce-scatter.11.cloned.1.call-start = ((), (), s32[]{:S(2)}) async-start(), calls=%async_computation.11 | async-start | bytes 2162688 | tf_op jit(solution)/shard_map/reduce_scatter | solution.py:177
  653.3 9.3 %copy-start.11 = (f32[128,256]{1,0:T(8,128)S(1)}, f32[128,256]{1,0:T(8,128)}, u32[]{:S(2)}) copy-start(f32[128,256]{1,0:T(8,128)} %get-tuple-element.108) | copy-start | bytes 393220
  658.3 5.9 copy-start.23
  660.8 8.7 %collective-permute-start.9 = (f32[128,2,64]{0,2,1:T(8,128)}, f32[128,2,64]{0,2,1:T(8,128)}, u32[]{:S(2)}, u32[]{:S(2)}) collective-permute-start(f32[128,2,64]{0,2,1:T(8,128)} %slice_select_fusion), channel_id=1, source_target_pairs={{0,4},{2,6},{4,0},{6,2},{8,12},{10,14},{12,8},{14,10},{16,20},{18,... | collective-permute-start | bytes 196616 | tf_op jit(solution)/shard_map/ppermute | solution.py:18
  664.3 5.1 copy-start.27
  664.4 6.6 copy-start.53
  664.4 6.6 copy-start.74
  664.4 6.6 copy-start.82
  670.4 2.0 collective-permute-start.10
  676.4 87.5 %copy-start.32 = (f32[128,128]{0,1:T(8,128)S(1)}, f32[128,128]{0,1:T(8,128)}, u32[]{:S(2)}) copy-start(f32[128,128]{0,1:T(8,128)} %reduce-scatter.5.cloned.1.call-done) | copy-start | bytes 196612
  676.4 87.5 %copy-start.33 = (f32[128,128]{0,1:T(8,128)S(1)}, f32[128,128]{0,1:T(8,128)}, u32[]{:S(2)}) copy-start(f32[128,128]{0,1:T(8,128)} %reduce-scatter.7.cloned.1.call-done) | copy-start | bytes 196612
  676.5 87.5 %copy-start.34 = (f32[128,128]{0,1:T(8,128)S(1)}, f32[128,128]{0,1:T(8,128)}, u32[]{:S(2)}) copy-start(f32[128,128]{0,1:T(8,128)} %reduce-scatter.9.cloned.1.call-done) | copy-start | bytes 196612
  (42 other events, 83.1 us)
Sparse Core Ops, SparseCore 0:
  9.8 56.3 all-gather.4
  107.4 87.0 reduce-scatter.4
  200.2 53.2 all-gather.6
  301.9 87.2 reduce-scatter.6
  395.0 53.2 all-gather.8
  496.7 87.1 reduce-scatter.8
  589.7 53.2 all-gather.10
  676.6 87.3 reduce-scatter.10
where the time goes:
time: 776 us; the launch traced here: 772 us
  waiting for transfers between devices  561 us (72%)
  matrix products  80.1 us (10%)
  other arithmetic  64 us (8%)
  local copies, waits for them, and re-layouts  42 us (5%)
  between operations  15 us (2%)
  starting transfers between devices  10 us (1%)
    reduce_scatter x4, waiting for transfers between devices, body(): lax.psum_scatter(summed + lax.dot_general(step_rows, grad_step, (((0,), (...  349 us
    all_gather x4, waiting for transfers between devices, body(): lax.all_gather(incoming, 'tensor', axis=1, tiled=True)  201 us
    dot_general x9, matrix products, state_space(): within = jnp.einsum('hcij,cjhp->cihp', weights, scaled, precision=HIGHEST)  21.1 us
    dot_general x4, matrix products, body(): lax.dot_general(main_cols, grad_main, (((1,), (1,)), ((), ())), preferred...  20.6 us
  transfers between devices with their start and end apart: 19, of which 11 were waited for; matrix products, arithmetic and copies ran while one was open for 9% of the time, Pallas kernels for 0%

commit v1 on v0

v1 whole, which is shorter than its diff:
```python
import jax
import jax.numpy as jnp
from jax import lax
from jax.experimental import pallas as pl
from jax.experimental.pallas import tpu as pltpu
from jax.sharding import PartitionSpec as P

F32 = jnp.float32
BF16 = jnp.bfloat16
HIGHEST = lax.Precision.HIGHEST
EPSILON = 1e-05
MESH = pl.DeviceIdType.MESH
NX = 4
NZ = 4
T = 128
FAR = (2, 1, 3, 0)


def nn(a, b, precision=None):
    return lax.dot_general(
        a, b, (((1,), (0,)), ((), ())), preferred_element_type=F32, precision=precision
    )


def nt(a, b, precision=None):
    return lax.dot_general(
        a, b, (((1,), (1,)), ((), ())), preferred_element_type=F32, precision=precision
    )


def shift_down(v, n, rows):
    if n == 0:
        return v
    return jnp.where(rows >= n, pltpu.roll(v, n, 0), 0.0)


def shift_up(v, n, rows):
    if n == 0:
        return v
    return jnp.where(rows < T - n, pltpu.roll(v, T - n, 0), 0.0)


def conv(v, taps, rows):
    out = taps[3:4] * v
    for k in range(3):
        out = out + taps[k : k + 1] * shift_down(v, 3 - k, rows)
    return out


def conv_back(v, taps, rows):
    out = taps[3:4] * v
    for k in range(3):
        out = out + taps[k : k + 1] * shift_up(v, 3 - k, rows)
    return out


def kernel(
    wm_hbm, ws_hbm, wt_hbm, wo_hbm,
    main_ref, state_ref, stepin_ref, vec_ref, cm_ref, cs_ref, gain_ref, og_ref,
    out_ref,
    WM, WO, WS, G, Q, PS, PR, RS, RR, XS, XR, ZS, ZR,
    NRM, SGI, YSP, MIX, STL, DSM, DSS, EM, SC, WTC, SCM, BC, SIG, L1, L2,
    wsem, ssem, rsem,
):
    s = lax.axis_index("pipe")
    t = lax.axis_index("tensor")
    x = t // 8
    z = (t // 2) % 4
    c = t % 2
    right_x = (x + 1) % NX
    left_x = (x + 3) % NX
    below = (s + 3) % 4
    above = (s + 1) % 4

    def place(px, pz, pc):
        return (px * NZ + pz) * 2 + pc

    def dev(tt, ss=None):
        if ss is None:
            return {"tensor": tt}
        return {"pipe": ss, "tensor": tt}

    count = [0]
    pending = []

    def remote(src, dst, target):
        i = count[0]
        count[0] += 1
        return pltpu.make_async_remote_copy(
            src_ref=src, dst_ref=dst, send_sem=ssem.at[i], recv_sem=rsem.at[i],
            device_id=target, device_id_type=MESH,
        )

    def go(copy):
        copy.start()
        pending.append(copy)
        return copy

    mate = dev(place(x, z, 1 - c))
    to_right = dev(place(right_x, z, c))
    to_left = dev(place(left_x, z, c))
    pair_z = z + 1 - 2 * (z % 2)
    to_pair = dev(place(x, pair_z, c))

    barrier = pltpu.get_barrier_semaphore()
    partners = [mate, to_right, to_left]
    for o in (1, 2, 3):
        partners.append(dev(place(x, (z + o) % NZ, c)))
    for o in range(4):
        partners.append(dev(place(x, (z + o) % NZ, c), below))
        partners.append(dev(place(x, (z + o) % NZ, c), above))
    for p in partners:
        pl.semaphore_signal(barrier, inc=1, device_id=p, device_id_type=MESH)

    m = t % 4
    loads = [
        pltpu.make_async_copy(wo_hbm.at[:, pl.ds(i * 256, 256)], WO.at[i], wsem.at[i])
        for i in range(16)
    ]
    loads.append(pltpu.make_async_copy(wm_hbm, WM, wsem.at[16]))
    own_b = pl.multiple_of(m * 32, 32)
    own_c = pl.multiple_of(128 + m * 32, 32)
    loads.append(pltpu.make_async_copy(ws_hbm.at[0], WS.at[pl.ds(own_b, 32)], wsem.at[17]))
    loads.append(pltpu.make_async_copy(ws_hbm.at[1], WS.at[pl.ds(own_c, 32)], wsem.at[18]))
    loads.append(pltpu.make_async_copy(wt_hbm, WS.at[256:384], wsem.at[19]))
    for load in loads:
        load.start()

    pl.semaphore_wait(barrier, len(partners))

    def hand_off(block, ids):
        copies = []
        for n, o in enumerate(FAR):
            slot = (4 - o) % 4
            copies.append(
                pltpu.make_async_remote_copy(
                    src_ref=block, dst_ref=G.at[c, 0, slot],
                    send_sem=ssem.at[ids[n]], recv_sem=rsem.at[ids[n]],
                    device_id=dev(place(x, (z + o) % NZ, c), below), device_id_type=MESH,
                )
            )
        return copies

    hand_ids = []
    for _ in range(4):
        hand_ids.append(count[0])
        count[0] += 1

    first = hand_off(og_ref, hand_ids)

    @pl.when(s == 0)
    def _():
        for copy in first:
            copy.start()

    mine = [
        remote(ws_hbm.at[0], WS.at[pl.ds(own_b, 32)], mate),
        remote(ws_hbm.at[1], WS.at[pl.ds(own_c, 32)], mate),
        remote(ws_hbm.at[0], WS.at[pl.ds(own_b, 32)], to_pair),
        remote(ws_hbm.at[1], WS.at[pl.ds(own_c, 32)], to_pair),
    ]
    for copy in mine:
        go(copy)
    far_b = pl.multiple_of(((m + 2) % 4) * 32, 32)
    far_c = pl.multiple_of(128 + ((m + 2) % 4) * 32, 32)
    passed = [
        remote(WS.at[pl.ds(far_b, 32)], WS.at[pl.ds(far_b, 32)], mate),
        remote(WS.at[pl.ds(far_c, 32)], WS.at[pl.ds(far_c, 32)], mate),
    ]

    rows = lax.broadcasted_iota(jnp.int32, (T, 256), 0)
    ri = lax.broadcasted_iota(jnp.int32, (T, T), 0)
    ci = lax.broadcasted_iota(jnp.int32, (T, T), 1)
    causal = ri >= ci
    rep = (
        lax.broadcasted_iota(jnp.int32, (T, 256), 0)
        == lax.broadcasted_iota(jnp.int32, (T, 256), 1) // 64
    ).astype(F32)
    gate = main_ref[:, 0:256].astype(F32)
    cm = cm_ref[...]
    cs = cs_ref[...]
    mixed = conv(main_ref[:, 256:512].astype(F32), cm, rows)
    sig = jax.nn.sigmoid(mixed)
    mix = mixed * sig
    DSM[...] = sig * (1.0 + mixed * (1.0 - sig))
    MIX[...] = mix
    states = conv(state_ref[...].astype(F32), cs, rows)
    sig = jax.nn.sigmoid(states)
    DSS[...] = sig * (1.0 + states * (1.0 - sig))
    states = states * sig
    BC[...] = states.astype(BF16)
    scores = nt(states[:, 128:256], states[:, 0:128], HIGHEST)
    SC[...] = scores
    vec = vec_ref[...]
    raw = stepin_ref[...] + vec[0:1]
    SIG[...] = jax.nn.sigmoid(raw)
    step = jnp.maximum(raw, 0.0) + jnp.log1p(jnp.exp(-jnp.abs(raw)))
    rate = -jnp.exp(vec[1:2])
    run_col = nn(causal.astype(F32), step * rate, HIGHEST)
    run_row = run_col.T
    stepl = nn(step, rep, HIGHEST)
    STL[...] = stepl
    skipl = nn(vec, rep, HIGHEST)[2:3]
    scaled = mix * stepl
    lane = lax.broadcasted_iota(jnp.int32, (T, T), 1)
    low = lane < 64
    ys = []
    for pair in range(2):
        sp = scaled[:, pair * 128 : pair * 128 + 128]
        acc = None
        for half in range(2):
            h = pair * 2 + half
            differ = run_col[:, h : h + 1] - run_row[h : h + 1, :]
            em = jnp.where(causal, jnp.exp(jnp.where(causal, differ, 0.0)), 0.0)
            EM[h] = em
            w = em * scores
            WTC[pair, :, half * 128 : half * 128 + 128] = w.T.astype(BF16)
            keep = low if half == 0 else jnp.logical_not(low)
            sh = jnp.where(keep, sp, 0.0)
            SCM[h] = sh.astype(BF16)
            part = nn(w, sh, HIGHEST)
            acc = part if acc is None else acc + part
        ys.append(acc)
    y = jnp.concatenate(ys, axis=1) + skipl * mix
    sg = jax.nn.sigmoid(gate)
    silu_gate = gate * sg
    gated = y * silu_gate
    inverse = lax.rsqrt(jnp.sum(gated * gated, axis=1, keepdims=True) * (1.0 / 256.0) + EPSILON)
    NRM[...] = gated * inverse
    SGI[...] = silu_gate * inverse
    YSP[...] = y * (sg * (1.0 + gate * (1.0 - sg))) * inverse

    ks = (0, 1, 3, 2)
    halves = (pl.ds(0, 64), pl.ds(64, 64))
    to_r = [remote(G.at[c, 0, k], G.at[c, 3, k], to_right) for k in range(4)]
    to_l = [remote(G.at[c, 0, k], G.at[c, 1, k], to_left) for k in range(4)]
    rel_r = [remote(G.at[c, 3, k, halves[0]], G.at[c, 2, k, halves[0]], to_right) for k in range(4)]
    rel_l = [remote(G.at[c, 1, k, halves[1]], G.at[c, 2, k, halves[1]], to_left) for k in range(4)]
    to_m = [[remote(G.at[c, j, k], G.at[c, j, k], mate) for k in range(4)] for j in range(4)]
    arrive = {}
    for n, o in enumerate(FAR):
        arrive[(4 - o) % 4] = first[n]

    for k in ks:
        arrive[k].wait_recv()
        go(to_r[k])
        go(to_l[k])
        go(to_m[0][k])
    for k in ks:
        to_r[k].wait_recv()
        go(rel_r[k])
        go(to_m[3][k])
        to_l[k].wait_recv()
        go(rel_l[k])
        go(to_m[1][k])
    for i in range(16):
        loads[i].wait()
    acc = None
    for j in (0, 3, 1, 2):
        for k in ks:
            if j == 2:
                rel_r[k].wait_recv()
                rel_l[k].wait_recv()
                go(to_m[2][k])
    for j in (0, 3, 1, 2):
        for k in ks:
            to_m[j][k].wait_recv()
            index = ((x + j) % NX) * NZ + (z + k) % NZ
            block = jnp.concatenate([G[0, j, k], G[1, j, k]], axis=1)
            part = nt(block, WO[index])
            acc = part if acc is None else acc + part

    dn = acc * gain_ref[...]
    nrm = NRM[...]
    mu = jnp.sum(dn * nrm, axis=1, keepdims=True) * (1.0 / 256.0)
    e = dn - nrm * mu
    dy = e * SGI[...]
    L1[:, 0:256] = (e * YSP[...]).astype(BF16)
    dyb = dy.astype(BF16)
    dscs = []
    ds = None
    masks = []
    for pair in range(2):
        dyp = dyb[:, pair * 128 : pair * 128 + 128]
        zero = jnp.zeros_like(dyp)
        both = jnp.concatenate([jnp.where(low, dyp, zero), jnp.where(low, zero, dyp)], axis=0)
        dscs.append(nn(WTC[pair], both))
        for half in range(2):
            h = pair * 2 + half
            a = nt(dyp, SCM[h]) * EM[h]
            ds = a if ds is None else ds + a
            masks.append((a * SC[...]).astype(BF16))
    dscaled = jnp.concatenate(dscs, axis=1)
    upper = (ci >= ri).astype(BF16)
    sums = nn(upper, jnp.concatenate(masks, axis=1))
    before = jnp.concatenate([ci < ri] * 4, axis=1)
    sums = jnp.where(before, sums, 0.0).astype(BF16)
    pick = (
        lax.broadcasted_iota(jnp.int32, (512, T), 0) // 128
        == lax.broadcasted_iota(jnp.int32, (512, T), 1)
    ).astype(BF16)
    ddecay = nn(sums, pick)
    pick64 = (
        lax.broadcasted_iota(jnp.int32, (256, T), 0) // 64
        == lax.broadcasted_iota(jnp.int32, (256, T), 1)
    ).astype(BF16)
    dstep = nn((dscaled * MIX[...]).astype(BF16), pick64)
    vec = vec_ref[...]
    dstep = dstep + ddecay * -jnp.exp(vec[1:2])
    L2[:, 256:384] = (dstep * SIG[...]).astype(BF16)
    skipl = nn(vec, rep, HIGHEST)[2:3]
    dmix = (dscaled * STL[...] + skipl * dy) * DSM[...]
    L1[:, 256:512] = conv_back(dmix, cm_ref[...], rows).astype(BF16)
    dsb = ds.astype(BF16)
    db = nn(ds.T.astype(BF16), BC[:, 128:256])
    dc = nn(dsb, BC[:, 0:128])
    dstate = jnp.concatenate([db, dc], axis=1) * DSS[...]
    L2[:, 0:256] = conv_back(dstate, cs_ref[...], rows).astype(BF16)

    mine[2].wait_recv()
    mine[3].wait_recv()
    for copy in passed:
        go(copy)
    mine[0].wait_recv()
    mine[1].wait_recv()
    for copy in passed:
        copy.wait_recv()
    for i in range(16, 20):
        loads[i].wait()

    lhs1 = L1[...]
    lhs2 = L2[...]
    first_core = c == 0
    to_mate = {}
    for j in FAR:
        for k in range(4):
            index = ((x + j) % NX) * NZ + (z + FAR[k]) % NZ
            at = pl.multiple_of(index * 256, 256)
            part = nt(lhs1, WM[pl.ds(at, 256), :]) + nn(lhs2, WS[:, pl.ds(at, 256)])
            lower, upper_half = part[:, 0:128], part[:, 128:256]
            Q[j, k] = jnp.where(first_core, lower, upper_half)
            PS[j, k] = jnp.where(first_core, upper_half, lower).astype(BF16)
            to_mate[j, k] = go(remote(PS.at[j, k], PR.at[j, k], mate))

    def chip_sum(j, k):
        to_mate[j, k].wait_recv()
        return Q[j, k] + PR[j, k].astype(F32)

    relays = {}
    for k in range(4):
        RS[k] = chip_sum(2, k).astype(BF16)
        relays[k] = go(remote(RS.at[k], RR.at[k], to_right if k % 2 == 0 else to_left))
    sends = {}

    def send_side(side, k, merged):
        value = chip_sum(1 if side == 0 else 3, k)
        if merged:
            relays[k].wait_recv()
            value = value + RR[k].astype(F32)
        XS[side, k] = value.astype(BF16)
        sends[side, k] = go(remote(XS.at[side, k], XR.at[side, k], to_right if side == 0 else to_left))

    for k in range(4):
        send_side(1 - k % 2, k, False) if k % 2 == 0 else send_side(0, k, False)
    for k in range(4):
        send_side(0 if k % 2 == 0 else 1, k, True)
    total = None
    zcopies = []
    for k in range(4):
        value = chip_sum(0, k)
        for side in range(2):
            sends[side, k].wait_recv()
            value = value + XR[side, k].astype(F32)
        if k < 3:
            ZS[k] = value.astype(BF16)
            zcopies.append(
                go(remote(ZS.at[k], ZR.at[k], dev(place(x, (z + FAR[k]) % NZ, c))))
            )
        else:
            total = value
    for k in (1, 2, 0):
        zcopies[k].wait_recv()
        total = total + ZR[k].astype(F32)
    out_ref[...] = total.astype(BF16)

    last = hand_off(out_ref, hand_ids)

    @pl.when(s > 0)
    def _():
        for copy in last:
            copy.start()

    for copy in last:
        copy.wait_send()
    for copy in pending:
        copy.wait_send()


N_COPIES = 4 + 4 + 2 + 16 + 16 + 16 + 4 + 8 + 3


def body(
    weight_main, weight_state, weight_step, weight_out, conv_main, conv_state, step_bias,
    decay_log, skip_gain, norm_gain, saved_main, saved_state, saved_step, output_grad,
):
    group = lax.axis_index("tensor") // 4
    wm = weight_main[0].reshape(4096, 512)
    ws = jnp.transpose(weight_state[0], (1, 2, 0))
    wt = jnp.pad(weight_step[0], ((0, 124), (0, 0)))
    main = saved_main[0].reshape(T, 512)
    state = lax.dynamic_slice_in_dim(saved_state[0], group * 128, 128, 2).reshape(T, 256)
    cs = lax.dynamic_slice_in_dim(conv_state[0], group * 128, 128, 2).reshape(4, 256)
    stepin = jnp.pad(saved_step[0].astype(F32).T, ((0, 0), (0, 124)))
    vec = jnp.pad(
        jnp.concatenate([step_bias, decay_log, skip_gain], axis=0), ((0, 5), (0, 124))
    )
    vmem = pl.BlockSpec(memory_space=pltpu.VMEM)
    hbm = pl.BlockSpec(memory_space=pl.ANY)
    block = (T, T)
    wide = (T, 256)
    result = pl.pallas_call(
        kernel,
        out_shape=jax.ShapeDtypeStruct((T, T), BF16),
        in_specs=[hbm] * 4 + [vmem] * 8,
        out_specs=vmem,
        scratch_shapes=[
            pltpu.VMEM((4096, 512), BF16),
            pltpu.VMEM((16, 256, 256), BF16),
            pltpu.VMEM((384, 4096), BF16),
            pltpu.VMEM((2, 4, 4) + block, BF16),
            pltpu.VMEM((4, 4) + block, F32),
            pltpu.VMEM((4, 4) + block, BF16),
            pltpu.VMEM((4, 4) + block, BF16),
            pltpu.VMEM((4,) + block, BF16),
            pltpu.VMEM((4,) + block, BF16),
            pltpu.VMEM((2, 4) + block, BF16),
            pltpu.VMEM((2, 4) + block, BF16),
            pltpu.VMEM((3,) + block, BF16),
            pltpu.VMEM((3,) + block, BF16),
            pltpu.VMEM(wide, F32),
            pltpu.VMEM(wide, F32),
            pltpu.VMEM(wide, F32),
            pltpu.VMEM(wide, F32),
            pltpu.VMEM(wide, F32),
            pltpu.VMEM(wide, F32),
            pltpu.VMEM(wide, F32),
            pltpu.VMEM((4,) + block, F32),
            pltpu.VMEM(block, F32),
            pltpu.VMEM((2, T, 256), BF16),
            pltpu.VMEM((4,) + block, BF16),
            pltpu.VMEM(wide, BF16),
            pltpu.VMEM(block, F32),
            pltpu.VMEM((T, 512), BF16),
            pltpu.VMEM((T, 384), BF16),
            pltpu.SemaphoreType.DMA((20,)),
            pltpu.SemaphoreType.DMA((N_COPIES + 16,)),
            pltpu.SemaphoreType.DMA((N_COPIES + 16,)),
        ],
        compiler_params=pltpu.CompilerParams(
            collective_id=0, has_side_effects=True, vmem_limit_bytes=48 * 1024 * 1024
        ),
        name="relay",
    )(wm, ws, wt, weight_out[0], main, state, stepin, vec, conv_main[0], cs, norm_gain, output_grad)
    return result[None]


def solution(mesh):
    return jax.shard_map(
        body,
        mesh=mesh,
        in_specs=(
            P("pipe", None, None, "tensor"),
            P("pipe", None, None, "tensor"),
            P("pipe", "tensor", None),
            P("pipe", "tensor", None),
            P("pipe", None, "tensor"),
            P("pipe", None, None, None),
            P("pipe", "tensor"),
            P("pipe", "tensor"),
            P("pipe", "tensor"),
            P("pipe", "tensor"),
            P("pipe", "dp", None, "tensor"),
            P("pipe", "dp", None, None),
            P("pipe", "tensor", "dp"),
            P("dp", "tensor"),
        ),
        out_specs=P("pipe", "dp", "tensor"),
        check_vma=False,
    )
```

time: 776 us -> 175 us (0.23)
  waiting for transfers between devices: 561 us -> 0 us
  Pallas kernels: 0 us -> 164 us
  matrix products: 80.1 us -> 0 us
  other arithmetic: 64 us -> 0.71 us
  local copies, waits for them, and re-layouts: 42 us -> 9.06 us
  between operations: 15 us -> 0.11 us
  starting transfers between devices: 10 us -> 0 us
    reduce_scatter x4 -> x0, waiting for transfers between devices: 349 us -> none  [body(): lax.psum_scatter(summed + lax.dot_general(step_rows, grad_step, (((0,), (...]
    all_gather x4 -> x0, waiting for transfers between devices: 201 us -> none  [body(): lax.all_gather(incoming, 'tensor', axis=1, tiled=True)]
    pallas_call x0 -> x1, Pallas kernels: none -> 164 us  [body(): pl.pallas_call(kernel, out_shape=jax.ShapeDtypeStruct((T, T), BF16), in_s...]
    dot_general x41 -> x0, matrix products: 80.1 us -> none  [the longest x9 21.1 us: state_space(): within = jnp.einsum('hcij,cjhp->cihp', weights, scaled, precision=HIGHEST)]
    mul x24 -> x0, other arithmetic: 20.3 us -> none  [the longest x16 14.3 us: causal_conv(): summed = summed + kernel[offset] * padded[offset:offset + length]]
    reshape x15 -> x0, local copies, waits for them, and re-layouts: 14.5 us -> none  [the longest x4 5.98 us: state_space(): (values * step_sizes.T[:, :, None]).reshape(blocks, STRETCH, head_count,...]
    mul x19 -> x0, local copies, waits for them, and re-layouts: 14.3 us -> none  [the longest x4 5.03 us: mamba_mixer(): gated = scanned.reshape(length, -1) * jax.nn.silu(gating)]
    convert_element_type x13 -> x0, other arithmetic: 10.6 us -> none  [the longest x4 3.87 us: body(): grad_main = back_grad_main.astype(jnp.bfloat16).reshape(length, -1)]
  transfers between devices with their start and end apart: 19 -> 0, of which waited for: 11 -> 0; matrix products, arithmetic and copies ran while one was open for 9% -> 0% of each run, Pallas kernels for 0% -> 0%
where the time goes in v1:
time: 175 us; the launch traced here: 174 us
  Pallas kernels  164 us (94%)
  local copies, waits for them, and re-layouts  9.06 us (5%)
    pallas_call x1, Pallas kernels, body(): pl.pallas_call(kernel, out_shape=jax.ShapeDtypeStruct((T, T), BF16), in_s...  164 us
    unnamed x19, local copies, waits for them, and re-layouts  8.15 us

profile of v1, /device:TPU:1, one launch (start us, length us, event | category | flops | bytes accessed | tf_op | source)
XLA Modules:
  0.0 174.4 jit_solution(12746406773942564065)
XLA Ops:
  0.0 0.0 copy-start
  0.0 0.7 dynamic-slice_bitcast_fusion
  0.8 0.7 select_maximum_fusion.vec_ref
  1.5 0.8 copy.15
  2.3 0.0 copy-done
  2.3 0.1 constant_dynamic-slice_fusion
  2.4 0.9 copy.17
  3.3 0.9 pad.14.wt_hbm
  4.2 0.0 copy-start.1
  4.2 0.0 copy-start.2
  4.2 0.0 copy-start.3
  4.2 0.0 copy-start.4
  4.2 0.0 copy-start.5
  4.2 5.0 %copy.16 = bf16[512,8,2,256]{3,1,2,0:T(8,128)(2,1)} copy(bf16[512,8,2,256]{3,2,1,0:T(2,128)(2,1)} %bitcast.35) | data formatting | bytes 8388608
  9.2 0.0 copy-done.1
  9.2 0.0 copy-done.2
  9.2 0.0 copy-done.3
  9.2 0.0 copy-done.4
  9.2 0.0 copy-done.5
  9.3 164.5 %relay.1 = bf16[128,128]{1,0:T(8,128)(2,1)S(1)} custom-call(bf16[4096,512]{1,0:T(8,128)(2,1)} %bitcast.34, bf16[2,32,4096]{2,1,0:T(8,128)(2,1)S(1)} %bitcast.29, bf16[128,4096]{1,0:T(8,128)(2,1)S(1)} %pad.14.wt_hbm, bf16[256,4096]{1,0:T(8,128)(2,1)S(1)} %bitcast.27, bf16[128,512]{1,0:T(8,128)(2,1)S(1)} %bitcast.28, bf16[128,256]{1,0:T(8,128)(2,1)S(1)} %bitcast.30, ...), custom_call_target="tpu_custom_call" | custom-call | tf_op jit(solution)/shard_map/relay/pallas_call | solution.py:421
  173.7 0.6 copy.25
  (3 shorter events, 0.0 us)
Async XLA Ops:
  0.0 2.3 %copy-start = (bf16[1,128,2,1024]{3,2,1,0:T(2,128)(2,1)S(1)}, bf16[1,128,2,1024]{3,2,1,0:T(2,128)(2,1)}, u32[]{:S(2)}) copy-start(bf16[1,128,2,1024]{3,2,1,0:T(2,128)(2,1)} %param.25) | copy-start | bytes 1572868
  4.2 5.1 %copy-start.1 = (bf16[1,256,4096]{2,1,0:T(8,128)(2,1)S(1)}, bf16[1,256,4096]{2,1,0:T(8,128)(2,1)}, u32[]{:S(2)}) copy-start(bf16[1,256,4096]{2,1,0:T(8,128)(2,1)} %param.17) | copy-start | bytes 6291460
  4.2 5.1 %copy-start.2 = (bf16[1,4096,2,32]{1,3,2,0:T(8,128)(2,1)S(1)}, bf16[1,4096,2,32]{1,3,2,0:T(8,128)(2,1)}, u32[]{:S(2)}) copy-start(bf16[1,4096,2,32]{1,3,2,0:T(8,128)(2,1)} %param.15) | copy-start | bytes 1572868
  4.2 5.1 %copy-start.3 = (bf16[128,128]{1,0:T(8,128)(2,1)S(1)}, bf16[128,128]{1,0:T(8,128)(2,1)}, u32[]{:S(2)}) copy-start(bf16[128,128]{1,0:T(8,128)(2,1)} %og_ref.1) | copy-start | bytes 98308
  4.2 5.0 %copy-start.4 = (f32[1,4,256]{2,1,0:T(4,128)S(1)}, f32[1,4,256]{2,1,0:T(4,128)}, u32[]{:S(2)}) copy-start(f32[1,4,256]{2,1,0:T(4,128)} %param.18) | copy-start | bytes 12292
  4.2 5.0 %copy-start.5 = (f32[1,256]{1,0:T(1,128)S(1)}, f32[1,256]{1,0:T(1,128)}, u32[]{:S(2)}) copy-start(f32[1,256]{1,0:T(1,128)} %gain_ref.1) | copy-start | bytes 3076

commit v2 on v1

v2 whole, which is shorter than its diff:
```python
import jax
import jax.numpy as jnp
from jax import lax
from jax.experimental import pallas as pl
from jax.experimental.pallas import tpu as pltpu
from jax.sharding import PartitionSpec as P

F32 = jnp.float32
BF16 = jnp.bfloat16
HIGHEST = lax.Precision.HIGHEST
EPSILON = 1e-05
MESH = pl.DeviceIdType.MESH
NX = 4
NZ = 4
T = 128
FAR = (2, 1, 3, 0)
H = 1
TH = T // H


def nn(a, b, precision=None):
    return lax.dot_general(
        a, b, (((1,), (0,)), ((), ())), preferred_element_type=F32, precision=precision
    )


def nt(a, b, precision=None):
    return lax.dot_general(
        a, b, (((1,), (1,)), ((), ())), preferred_element_type=F32, precision=precision
    )


def shift_down(v, n, rows):
    if n == 0:
        return v
    return jnp.where(rows >= n, pltpu.roll(v, n, 0), 0.0)


def shift_up(v, n, rows):
    if n == 0:
        return v
    return jnp.where(rows < T - n, pltpu.roll(v, T - n, 0), 0.0)


def conv(v, taps, rows):
    out = taps[3:4] * v
    for k in range(3):
        out = out + taps[k : k + 1] * shift_down(v, 3 - k, rows)
    return out


def conv_back(v, taps, rows):
    out = taps[3:4] * v
    for k in range(3):
        out = out + taps[k : k + 1] * shift_up(v, 3 - k, rows)
    return out


def kernel(
    wm_hbm, ws_hbm, wo_hbm,
    wt_ref, main_ref, state_ref, stepin_ref, vec_ref, cm_ref, cs_ref, gain_ref, og_ref,
    out_ref,
    WM, WO, WS, G, Q, PS, PR, XS, XR, ZS, ZR,
    NRM, SGI, YSP, MIX, STL, DSM, DSS, EM, SC, WTC, SCM, BC, SIG, SK, L1, L2, AS, AR, PM,
    wsem, ssem, rsem,
):
    s = lax.axis_index("pipe")
    t = lax.axis_index("tensor")
    x = t // 8
    z = (t // 2) % 4
    c = t % 2
    right_x = (x + 1) % NX
    left_x = (x + 3) % NX
    below = (s + 3) % 4
    above = (s + 1) % 4

    def place(px, pz, pc):
        return (px * NZ + pz) * 2 + pc

    def dev(tt, ss=None):
        if ss is None:
            return {"tensor": tt}
        return {"pipe": ss, "tensor": tt}

    count = [0]
    pending = []

    def remote(src, dst, target):
        i = count[0]
        count[0] += 1
        return pltpu.make_async_remote_copy(
            src_ref=src, dst_ref=dst, send_sem=ssem.at[i], recv_sem=rsem.at[i],
            device_id=target, device_id_type=MESH,
        )

    def go(copy):
        copy.start()
        pending.append(copy)
        return copy

    mate = dev(place(x, z, 1 - c))
    to_right = dev(place(right_x, z, c))
    to_left = dev(place(left_x, z, c))
    to_opposite = dev(place((x + 2) % NX, z, c))
    pair_z = z + 1 - 2 * (z % 2)
    to_pair = dev(place(x, pair_z, c))

    barrier = pltpu.get_barrier_semaphore()
    partners = [mate, to_right, to_left, to_opposite]
    for o in (1, 2, 3):
        partners.append(dev(place(x, (z + o) % NZ, c)))
    for o in range(4):
        partners.append(dev(place(x, (z + o) % NZ, c), below))
        partners.append(dev(place(x, (z + o) % NZ, c), above))
    for p in partners:
        pl.semaphore_signal(barrier, inc=1, device_id=p, device_id_type=MESH)

    loads = [
        pltpu.make_async_copy(wo_hbm.at[:, pl.ds(i * 256, 256)], WO.at[i], wsem.at[i])
        for i in range(16)
    ]
    loads.append(pltpu.make_async_copy(wm_hbm, WM, wsem.at[16]))
    own_b = pl.ds(pl.multiple_of(c * 32, 32), 32)
    own_c = pl.ds(pl.multiple_of(64 + c * 32, 32), 32)
    loads.append(pltpu.make_async_copy(ws_hbm.at[0], WS.at[own_b], wsem.at[17]))
    loads.append(pltpu.make_async_copy(ws_hbm.at[1], WS.at[own_c], wsem.at[18]))
    for load in loads:
        load.start()

    pl.semaphore_wait(barrier, len(partners))

    pieces = [pl.ds(h * TH, TH) for h in range(H)]
    hand_ids = list(range(count[0], count[0] + 4 * H))
    count[0] += 4 * H

    def hand_off(block, h):
        copies = []
        for n, o in enumerate(FAR):
            i = hand_ids[4 * h + n]
            copies.append(
                pltpu.make_async_remote_copy(
                    src_ref=block.at[pieces[h]], dst_ref=G.at[c, 0, (4 - o) % 4, pieces[h]],
                    send_sem=ssem.at[i], recv_sem=rsem.at[i],
                    device_id=dev(place(x, (z + o) % NZ, c), below), device_id_type=MESH,
                )
            )
        return copies

    first = [hand_off(og_ref, h) for h in range(H)]

    @pl.when(s == 0)
    def _():
        for copies in first:
            for copy in copies:
                copy.start()

    mine = [
        go(remote(ws_hbm.at[0], WS.at[own_b], mate)),
        go(remote(ws_hbm.at[1], WS.at[own_c], mate)),
    ]
    WS[128:256, :] = jnp.zeros((128, 4096), BF16)
    WS[128:132, :] = wt_ref[...]

    rows = lax.broadcasted_iota(jnp.int32, (T, 256), 0)
    ri = lax.broadcasted_iota(jnp.int32, (T, T), 0)
    ci = lax.broadcasted_iota(jnp.int32, (T, T), 1)
    causal = ri >= ci
    rep = (
        lax.broadcasted_iota(jnp.int32, (T, 256), 0)
        == lax.broadcasted_iota(jnp.int32, (T, 256), 1) // 64
    ).astype(F32)
    gate = main_ref[:, 0:256].astype(F32)
    cm = cm_ref[...]
    cs = cs_ref[...]
    mixed = conv(main_ref[:, 256:512].astype(F32), cm, rows)
    sig = jax.nn.sigmoid(mixed)
    mix = mixed * sig
    DSM[...] = sig * (1.0 + mixed * (1.0 - sig))
    MIX[...] = mix
    states = conv(state_ref[...].astype(F32), cs, rows)
    sig = jax.nn.sigmoid(states)
    DSS[...] = sig * (1.0 + states * (1.0 - sig))
    states = states * sig
    BC[...] = states.astype(BF16)
    scores = nt(states[:, 128:256], states[:, 0:128], HIGHEST)
    SC[...] = scores
    vec = vec_ref[...]
    raw = stepin_ref[...] + vec[0:1]
    SIG[...] = jax.nn.sigmoid(raw)
    step = jnp.maximum(raw, 0.0) + jnp.log1p(jnp.exp(-jnp.abs(raw)))
    rate = -jnp.exp(vec[1:2])
    run_col = nn(causal.astype(F32), step * rate, HIGHEST)
    run_row = run_col.T
    stepl = nn(step, rep, HIGHEST)
    STL[...] = stepl
    SK[...] = nn(vec, rep, HIGHEST)
    skipl = SK[2:3]
    scaled = mix * stepl
    low = ci < 64
    ys = []
    for pair in range(2):
        sp = scaled[:, pair * 128 : pair * 128 + 128]
        acc = None
        for half in range(2):
            h = pair * 2 + half
            differ = run_col[:, h : h + 1] - run_row[h : h + 1, :]
            em = jnp.where(causal, jnp.exp(jnp.where(causal, differ, 0.0)), 0.0)
            EM[h] = em
            w = em * scores
            WTC[pair, :, half * 128 : half * 128 + 128] = w.T.astype(BF16)
            keep = low if half == 0 else jnp.logical_not(low)
            sh = jnp.where(keep, sp, 0.0)
            SCM[h] = sh.astype(BF16)
            part = nn(w, sh, HIGHEST)
            acc = part if acc is None else acc + part
        ys.append(acc)
    y = jnp.concatenate(ys, axis=1) + skipl * mix
    sg = jax.nn.sigmoid(gate)
    silu_gate = gate * sg
    gated = y * silu_gate
    inverse = lax.rsqrt(jnp.sum(gated * gated, axis=1, keepdims=True) * (1.0 / 256.0) + EPSILON)
    NRM[...] = gated * inverse
    SGI[...] = silu_gate * inverse
    YSP[...] = y * (sg * (1.0 + gate * (1.0 - sg))) * inverse

    ks = (0, 1, 3, 2)

    def spread(src_j, dst_j, target, h, k):
        return remote(G.at[c, src_j, k, pieces[h]], G.at[c, dst_j, k, pieces[h]], target)

    grid = [(h, k) for h in range(H) for k in ks]
    to_r = {hk: spread(0, 3, to_right, *hk) for hk in grid}
    to_l = {hk: spread(0, 1, to_left, *hk) for hk in grid}
    to_o = {hk: spread(0, 2, to_opposite, *hk) for hk in grid}
    to_m = {(j, h, k): spread(j, j, mate, h, k) for j in range(4) for h, k in grid}

    for h, k in grid:
        first[h][FAR.index((4 - k) % 4)].wait_recv()
        go(to_o[h, k])
        go(to_r[h, k])
        go(to_l[h, k])
        go(to_m[0, h, k])
    for h, k in grid:
        to_r[h, k].wait_recv()
        go(to_m[3, h, k])
        to_l[h, k].wait_recv()
        go(to_m[1, h, k])
    for i in range(16):
        loads[i].wait()
    totals = [None]

    def multiply(j):
        for k in ks:
            for h in range(H):
                to_m[j, h, k].wait_recv()
            index = ((x + j) % NX) * NZ + (z + k) % NZ
            block = jnp.concatenate([G[0, j, k], G[1, j, k]], axis=1)
            part = nt(block, WO[index])
            totals[0] = part if totals[0] is None else totals[0] + part

    multiply(0)
    multiply(3)
    for h, k in grid:
        to_o[h, k].wait_recv()
        go(to_m[2, h, k])
    multiply(1)
    multiply(2)
    acc = totals[0]

    dn = acc * gain_ref[...]
    nrm = NRM[...]
    mu = jnp.sum(dn * nrm, axis=1, keepdims=True) * (1.0 / 256.0)
    e = dn - nrm * mu
    dy = e * SGI[...]
    L1[:, 0:256] = (e * YSP[...]).astype(BF16)
    dyb = dy.astype(BF16)
    ds = None
    masks = []
    for h in range(4):
        a = nt(dyb[:, h // 2 * 128 : h // 2 * 128 + 128], SCM[h]) * EM[h]
        ds = a if ds is None else ds + a
        masks.append((a * SC[...]).astype(BF16))
    db = nn(ds.T.astype(BF16), BC[:, 128:256])
    dc = nn(ds.astype(BF16), BC[:, 0:128])
    dstate = conv_back(jnp.concatenate([db, dc], axis=1) * DSS[...], cs_ref[...], rows)
    db, dc = dstate[:, 0:128], dstate[:, 128:256]
    near = jnp.where(low, db, pltpu.roll(dc, 64, 1))
    far = jnp.where(low, pltpu.roll(db, 64, 1), dc)
    even = z % 2 == 0
    own_state = jnp.where(even, near, far)
    AS[...] = jnp.where(even, far, near).astype(BF16)
    swap = go(remote(AS, AR, to_pair))
    dscs = []
    for pair in range(2):
        dyp = dyb[:, pair * 128 : pair * 128 + 128]
        zero = jnp.zeros_like(dyp)
        both = jnp.concatenate([jnp.where(low, dyp, zero), jnp.where(low, zero, dyp)], axis=0)
        dscs.append(nn(WTC[pair], both))
    dscaled = jnp.concatenate(dscs, axis=1)
    dmix = (dscaled * STL[...] + SK[2:3] * dy) * DSM[...]
    L1[:, 256:512] = conv_back(dmix, cm_ref[...], rows).astype(BF16)
    upper = (ci >= ri).astype(BF16)
    sums = nn(upper, jnp.concatenate(masks, axis=1))
    before = jnp.concatenate([ci < ri] * 4, axis=1)
    sums = jnp.where(before, sums, 0.0).astype(BF16)
    pick = (
        lax.broadcasted_iota(jnp.int32, (512, T), 0) // 128
        == lax.broadcasted_iota(jnp.int32, (512, T), 1)
    ).astype(BF16)
    ddecay = nn(sums, pick)
    pick64 = (
        lax.broadcasted_iota(jnp.int32, (256, T), 0) // 64
        == lax.broadcasted_iota(jnp.int32, (256, T), 1)
    ).astype(BF16)
    dstep = nn((dscaled * MIX[...]).astype(BF16), pick64)
    dstep = dstep + ddecay * -jnp.exp(vec_ref[1:2])
    L2[:, 128:256] = (dstep * SIG[...]).astype(BF16)

    loads[16].wait()
    lhs1 = L1[...]
    places = {}
    for j in FAR:
        for k in range(4):
            index = ((x + j) % NX) * NZ + (z + FAR[k]) % NZ
            places[j, k] = pl.ds(pl.multiple_of(index * 256, 256), 256)
            PM[j, k] = nt(lhs1, WM[places[j, k], :])
    loads[17].wait()
    loads[18].wait()
    for copy in mine:
        copy.wait_recv()
    swap.wait_recv()
    L2[:, 0:128] = (own_state + AR[...].astype(F32)).astype(BF16)
    lhs2 = L2[...]
    first_core = c == 0
    to_mate = {}
    for k in range(4):
        for j in FAR:
            part = PM[j, k] + nn(lhs2, WS[:, places[j, k]])
            lower, upper_half = part[:, 0:128], part[:, 128:256]
            Q[j, k] = jnp.where(first_core, lower, upper_half)
            PS[j, k] = jnp.where(first_core, upper_half, lower).astype(BF16)
            to_mate[j, k] = go(remote(PS.at[j, k], PR.at[j, k], mate))

    arrived = set()

    def chip_sum(j, k, h):
        if (j, k) not in arrived:
            arrived.add((j, k))
            to_mate[j, k].wait_recv()
        return Q[j, k, pieces[h]] + PR[j, k, pieces[h]].astype(F32)

    sends = {}
    zcopies = {}
    totals = {}
    sides = ((2, to_opposite), (1, to_right), (3, to_left))

    def send_x(h, k):
        for n, (j, target) in enumerate(sides):
            XS[n, k, pieces[h]] = chip_sum(j, k, h).astype(BF16)
            sends[n, h, k] = go(remote(XS.at[n, k, pieces[h]], XR.at[n, k, pieces[h]], target))

    def send_z(h, k):
        value = chip_sum(0, k, h)
        for n in (1, 2, 0):
            sends[n, h, k].wait_recv()
            value = value + XR[n, k, pieces[h]].astype(F32)
        if k < 3:
            ZS[k, pieces[h]] = value.astype(BF16)
            zcopies[h, k] = go(
                remote(
                    ZS.at[k, pieces[h]], ZR.at[k, pieces[h]],
                    dev(place(x, (z + FAR[k]) % NZ, c)),
                )
            )
        else:
            totals[h] = value

    for h in range(H):
        for k in range(4):
            send_x(h, k)
    for h in range(H):
        for k in range(4):
            send_z(h, k)
    for h in range(H):
        total = totals[h]
        for k in (1, 2, 0):
            zcopies[h, k].wait_recv()
            total = total + ZR[k, pieces[h]].astype(F32)
        out_ref[pieces[h], :] = total.astype(BF16)
        last = hand_off(out_ref, h)

        @pl.when(s > 0)
        def _():
            for copy in last:
                copy.start()

    for copies in first:
        for copy in copies:
            copy.wait_send()
    for copy in pending:
        copy.wait_send()


N_COPIES = H * (4 + 12 + 16 + 12 + 3) + 2 + 1 + 16


def body(
    weight_main, weight_state, weight_step, weight_out, conv_main, conv_state, step_bias,
    decay_log, skip_gain, norm_gain, saved_main, saved_state, saved_step, output_grad,
):
    group = lax.axis_index("tensor") // 4
    wm = weight_main[0].reshape(4096, 512)
    ws = jnp.transpose(weight_state[0], (1, 2, 0))
    main = saved_main[0].reshape(T, 512)
    state = lax.dynamic_slice_in_dim(saved_state[0], group * 128, 128, 2).reshape(T, 256)
    cs = lax.dynamic_slice_in_dim(conv_state[0], group * 128, 128, 2).reshape(4, 256)
    stepin = jnp.pad(saved_step[0].astype(F32).T, ((0, 0), (0, 124)))
    vec = jnp.pad(
        jnp.concatenate([step_bias, decay_log, skip_gain], axis=0), ((0, 5), (0, 124))
    )
    vmem = pl.BlockSpec(memory_space=pltpu.VMEM)
    hbm = pl.BlockSpec(memory_space=pl.ANY)
    block = (T, T)
    wide = (T, 256)
    result = pl.pallas_call(
        kernel,
        out_shape=jax.ShapeDtypeStruct((T, T), BF16),
        in_specs=[hbm] * 3 + [vmem] * 9,
        out_specs=vmem,
        scratch_shapes=[
            pltpu.VMEM((4096, 512), BF16),
            pltpu.VMEM((16, 256, 256), BF16),
            pltpu.VMEM((256, 4096), BF16),
            pltpu.VMEM((2, 4, 4) + block, BF16),
            pltpu.VMEM((4, 4) + block, F32),
            pltpu.VMEM((4, 4) + block, BF16),
            pltpu.VMEM((4, 4) + block, BF16),
            pltpu.VMEM((3, 4) + block, BF16),
            pltpu.VMEM((3, 4) + block, BF16),
            pltpu.VMEM((3,) + block, BF16),
            pltpu.VMEM((3,) + block, BF16),
            pltpu.VMEM(wide, F32),
            pltpu.VMEM(wide, F32),
            pltpu.VMEM(wide, F32),
            pltpu.VMEM(wide, F32),
            pltpu.VMEM(wide, F32),
            pltpu.VMEM(wide, F32),
            pltpu.VMEM(wide, F32),
            pltpu.VMEM((4,) + block, F32),
            pltpu.VMEM(block, F32),
            pltpu.VMEM((2, T, 256), BF16),
            pltpu.VMEM((4,) + block, BF16),
            pltpu.VMEM(wide, BF16),
            pltpu.VMEM(block, F32),
            pltpu.VMEM((8, 256), F32),
            pltpu.VMEM((T, 512), BF16),
            pltpu.VMEM((T, 256), BF16),
            pltpu.VMEM(block, BF16),
            pltpu.VMEM(block, BF16),
            pltpu.VMEM((4, 4, T, 256), F32),
            pltpu.SemaphoreType.DMA((20,)),
            pltpu.SemaphoreType.DMA((N_COPIES,)),
            pltpu.SemaphoreType.DMA((N_COPIES,)),
        ],
        compiler_params=pltpu.CompilerParams(
            collective_id=0, has_side_effects=True, vmem_limit_bytes=48 * 1024 * 1024
        ),
        name="relay",
    )(wm, ws, weight_out[0], weight_step[0], main, state, stepin, vec, conv_main[0], cs, norm_gain, output_grad)
    return result[None]


def solution(mesh):
    return jax.shard_map(
        body,
        mesh=mesh,
        in_specs=(
            P("pipe", None, None, "tensor"),
            P("pipe", None, None, "tensor"),
            P("pipe", "tensor", None),
            P("pipe", "tensor", None),
            P("pipe", None, "tensor"),
            P("pipe", None, None, None),
            P("pipe", "tensor"),
            P("pipe", "tensor"),
            P("pipe", "tensor"),
            P("pipe", "tensor"),
            P("pipe", "dp", None, "tensor"),
            P("pipe", "dp", None, None),
            P("pipe", "tensor", "dp"),
            P("dp", "tensor"),
        ),
        out_specs=P("pipe", "dp", "tensor"),
        check_vma=False,
    )
```

time: 175 us -> 144 us (0.82)
  Pallas kernels: 164 us -> 133 us
    pallas_call x1, Pallas kernels: 164 us -> 133 us  [body(): pl.pallas_call(kernel, out_shape=jax.ShapeDtypeStruct((T, T), BF16), in_s...]
    unnamed x19 -> x21, local copies, waits for them, and re-layouts: 8.15 us -> 8.17 us
where the time goes in v2:
time: 144 us; the launch traced here: 142 us
  Pallas kernels  133 us (92%)
  local copies, waits for them, and re-layouts  8.23 us (6%)
    pallas_call x1, Pallas kernels, body(): pl.pallas_call(kernel, out_shape=jax.ShapeDtypeStruct((T, T), BF16), in_s...  133 us
    unnamed x21, local copies, waits for them, and re-layouts  8.17 us

profile of v2, /device:TPU:1, one launch (start us, length us, event | category | flops | bytes accessed | tf_op | source)
XLA Modules:
  0.0 142.4 jit_solution(13340720447848587776)
XLA Ops:
  0.0 0.0 copy-start
  0.0 0.7 dynamic-slice_bitcast_fusion
  0.8 0.7 select_maximum_fusion.vec_ref
  1.5 0.8 copy.15
  2.3 0.0 copy-done
  2.3 0.1 constant_dynamic-slice_fusion
  2.4 0.9 copy.17
  3.3 0.0 copy-start.1
  3.3 0.0 copy-start.2
  3.3 0.0 copy-start.3
  3.3 0.0 copy-start.4
  3.3 0.0 copy-start.5
  3.4 0.0 copy-start.6
  3.4 5.0 %copy.16 = bf16[512,8,2,256]{3,1,2,0:T(8,128)(2,1)} copy(bf16[512,8,2,256]{3,2,1,0:T(2,128)(2,1)} %bitcast.36) | data formatting | bytes 8388608
  8.4 0.0 copy-done.1
  8.4 0.0 copy-done.2
  8.4 0.0 copy-done.3
  8.4 0.0 copy-done.4
  8.4 0.0 copy-done.5
  8.4 0.0 copy-done.6
  8.4 133.4 %relay.1 = bf16[128,128]{1,0:T(8,128)(2,1)S(1)} custom-call(bf16[4096,512]{1,0:T(8,128)(2,1)} %bitcast.35, bf16[2,32,4096]{2,1,0:T(8,128)(2,1)S(1)} %bitcast.29, bf16[256,4096]{1,0:T(8,128)(2,1)S(1)} %bitcast.27, bf16[4,4096]{1,0:T(4,128)(2,1)S(1)} %bitcast.32, bf16[128,512]{1,0:T(8,128)(2,1)S(1)} %bitcast.28, bf16[128,256]{1,0:T(8,128)(2,1)S(1)} %bitcast.30, ...), custom_call_target="tpu_custom_call" | custom-call | tf_op jit(solution)/shard_map/relay/pallas_call | solution.py:425
  141.8 0.6 copy.25
  (3 shorter events, 0.0 us)
Async XLA Ops:
  0.0 2.3 %copy-start = (bf16[1,128,2,1024]{3,2,1,0:T(2,128)(2,1)S(1)}, bf16[1,128,2,1024]{3,2,1,0:T(2,128)(2,1)}, u32[]{:S(2)}) copy-start(bf16[1,128,2,1024]{3,2,1,0:T(2,128)(2,1)} %param.25) | copy-start | bytes 1572868
  3.3 5.1 %copy-start.1 = (bf16[1,256,4096]{2,1,0:T(8,128)(2,1)S(1)}, bf16[1,256,4096]{2,1,0:T(8,128)(2,1)}, u32[]{:S(2)}) copy-start(bf16[1,256,4096]{2,1,0:T(8,128)(2,1)} %param.17) | copy-start | bytes 6291460
  3.3 5.1 %copy-start.2 = (bf16[1,4096,2,32]{1,3,2,0:T(8,128)(2,1)S(1)}, bf16[1,4096,2,32]{1,3,2,0:T(8,128)(2,1)}, u32[]{:S(2)}) copy-start(bf16[1,4096,2,32]{1,3,2,0:T(8,128)(2,1)} %param.15) | copy-start | bytes 1572868
  3.3 5.1 %copy-start.3 = (bf16[1,4,4096]{2,1,0:T(4,128)(2,1)S(1)}, bf16[1,4,4096]{2,1,0:T(4,128)(2,1)}, u32[]{:S(2)}) copy-start(bf16[1,4,4096]{2,1,0:T(4,128)(2,1)} %param.16) | copy-start | bytes 98308
  3.3 5.1 %copy-start.4 = (bf16[128,128]{1,0:T(8,128)(2,1)S(1)}, bf16[128,128]{1,0:T(8,128)(2,1)}, u32[]{:S(2)}) copy-start(bf16[128,128]{1,0:T(8,128)(2,1)} %og_ref.1) | copy-start | bytes 98308
  3.3 5.1 %copy-start.5 = (f32[1,4,256]{2,1,0:T(4,128)S(1)}, f32[1,4,256]{2,1,0:T(4,128)}, u32[]{:S(2)}) copy-start(f32[1,4,256]{2,1,0:T(4,128)} %param.18) | copy-start | bytes 12292
  3.4 5.1 %copy-start.6 = (f32[1,256]{1,0:T(1,128)S(1)}, f32[1,256]{1,0:T(1,128)}, u32[]{:S(2)}) copy-start(f32[1,256]{1,0:T(1,128)} %gain_ref.1) | copy-start | bytes 3076

commit v3 on v2

--- a/solution.py
+++ b/solution.py
@@ -61,7 +61,7 @@
     wt_ref, main_ref, state_ref, stepin_ref, vec_ref, cm_ref, cs_ref, gain_ref, og_ref,
     out_ref,
     WM, WO, WS, G, Q, PS, PR, XS, XR, ZS, ZR,
-    NRM, SGI, YSP, MIX, STL, DSM, DSS, EM, SC, WTC, SCM, BC, SIG, SK, L1, L2, AS, AR, PM,
+    NRM, SGI, YSP, MIX, STL, DSM, DSS, EM, SC, WTC, SCM, BC, SIG, SK, L1, L2,
     wsem, ssem, rsem,
 ):
     s = lax.axis_index("pipe")
@@ -69,6 +69,7 @@
     x = t // 8
     z = (t // 2) % 4
     c = t % 2
+    d = lax.axis_index("dp")
     right_x = (x + 1) % NX
     left_x = (x + 3) % NX
     below = (s + 3) % 4
@@ -103,10 +104,12 @@
     to_left = dev(place(left_x, z, c))
     to_opposite = dev(place((x + 2) % NX, z, c))
     pair_z = z + 1 - 2 * (z % 2)
-    to_pair = dev(place(x, pair_z, c))
+    inner = z % 2 != d
+    to_inner = {"tensor": place(x, pair_z, c), "dp": 1 - d}
+    to_outer = {"tensor": t, "dp": 1 - d}
 
     barrier = pltpu.get_barrier_semaphore()
-    partners = [mate, to_right, to_left, to_opposite]
+    partners = [mate, to_right, to_left, to_opposite, to_inner, to_outer]
     for o in (1, 2, 3):
         partners.append(dev(place(x, (z + o) % NZ, c)))
     for o in range(4):
@@ -120,10 +123,19 @@
         for i in range(16)
     ]
     loads.append(pltpu.make_async_copy(wm_hbm, WM, wsem.at[16]))
-    own_b = pl.ds(pl.multiple_of(c * 32, 32), 32)
-    own_c = pl.ds(pl.multiple_of(64 + c * 32, 32), 32)
-    loads.append(pltpu.make_async_copy(ws_hbm.at[0], WS.at[own_b], wsem.at[17]))
-    loads.append(pltpu.make_async_copy(ws_hbm.at[1], WS.at[own_c], wsem.at[18]))
+    m = t % 4
+    cuts = [(half, pl.ds(part * 2048, 2048)) for half in range(2) for part in range(2)]
+
+    def columns(member, half, lanes):
+        return WS.at[pl.ds(pl.multiple_of(half * 128 + member * 32, 32), 32), lanes]
+
+    def own_columns(half, lanes):
+        return ws_hbm.at[half, :, lanes]
+
+    loads += [
+        pltpu.make_async_copy(own_columns(*cut), columns(m, *cut), wsem.at[17 + q])
+        for q, cut in enumerate(cuts)
+    ]
     for load in loads:
         load.start()
 
@@ -154,12 +166,31 @@
             for copy in copies:
                 copy.start()
 
-    mine = [
-        go(remote(ws_hbm.at[0], WS.at[own_b], mate)),
-        go(remote(ws_hbm.at[1], WS.at[own_c], mate)),
-    ]
-    WS[128:256, :] = jnp.zeros((128, 4096), BF16)
-    WS[128:132, :] = wt_ref[...]
+    mine = [go(remote(own_columns(*cut), columns(m, *cut), mate)) for cut in cuts]
+    swaps = [remote(own_columns(*cut), columns(m, *cut), to_inner) for cut in cuts]
+    other = (m + 2) % 4
+    passes = [remote(columns(other, *cut), columns(other, *cut), to_outer) for cut in cuts]
+    shares = [remote(columns(other, *cut), columns(other, *cut), mate) for cut in cuts]
+
+    @pl.when(inner)
+    def _():
+        for copy in swaps:
+            copy.start()
+
+    def relay(chosen):
+        for q in chosen:
+            swaps[q].wait_recv()
+            passes[q].start()
+            shares[q].start()
+
+    def accept():
+        for q in range(4):
+            passes[q].wait_recv()
+            shares[q].start()
+
+    early = s != 3
+    WS[256:384, :] = jnp.zeros((128, 4096), BF16)
+    WS[256:260, :] = wt_ref[...]
 
     rows = lax.broadcasted_iota(jnp.int32, (T, 256), 0)
     ri = lax.broadcasted_iota(jnp.int32, (T, T), 0)
@@ -234,17 +265,35 @@
     to_o = {hk: spread(0, 2, to_opposite, *hk) for hk in grid}
     to_m = {(j, h, k): spread(j, j, mate, h, k) for j in range(4) for h, k in grid}
 
+    @pl.when(jnp.logical_and(early, inner))
+    def _():
+        relay(range(4))
+
+    @pl.when(jnp.logical_and(early, jnp.logical_not(inner)))
+    def _():
+        accept()
+
     for h, k in grid:
         first[h][FAR.index((4 - k) % 4)].wait_recv()
         go(to_o[h, k])
         go(to_r[h, k])
         go(to_l[h, k])
         go(to_m[0, h, k])
+
+    @pl.when(jnp.logical_and(s == 3, inner))
+    def _():
+        relay((0, 1))
+
     for h, k in grid:
         to_r[h, k].wait_recv()
         go(to_m[3, h, k])
         to_l[h, k].wait_recv()
         go(to_m[1, h, k])
+
+    @pl.when(jnp.logical_and(s == 3, inner))
+    def _():
+        relay((2, 3))
+
     for i in range(16):
         loads[i].wait()
     totals = [None]
@@ -282,14 +331,8 @@
         masks.append((a * SC[...]).astype(BF16))
     db = nn(ds.T.astype(BF16), BC[:, 128:256])
     dc = nn(ds.astype(BF16), BC[:, 0:128])
-    dstate = conv_back(jnp.concatenate([db, dc], axis=1) * DSS[...], cs_ref[...], rows)
-    db, dc = dstate[:, 0:128], dstate[:, 128:256]
-    near = jnp.where(low, db, pltpu.roll(dc, 64, 1))
-    far = jnp.where(low, pltpu.roll(db, 64, 1), dc)
-    even = z % 2 == 0
-    own_state = jnp.where(even, near, far)
-    AS[...] = jnp.where(even, far, near).astype(BF16)
-    swap = go(remote(AS, AR, to_pair))
+    dstate = jnp.concatenate([db, dc], axis=1) * DSS[...]
+    L2[:, 0:256] = conv_back(dstate, cs_ref[...], rows).astype(BF16)
     dscs = []
     for pair in range(2):
         dyp = dyb[:, pair * 128 : pair * 128 + 128]
@@ -314,32 +357,29 @@
     ).astype(BF16)
     dstep = nn((dscaled * MIX[...]).astype(BF16), pick64)
     dstep = dstep + ddecay * -jnp.exp(vec_ref[1:2])
-    L2[:, 128:256] = (dstep * SIG[...]).astype(BF16)
-
-    loads[16].wait()
+    L2[:, 256:384] = (dstep * SIG[...]).astype(BF16)
+
+    @pl.when(jnp.logical_and(s == 3, jnp.logical_not(inner)))
+    def _():
+        accept()
+
+    for load in loads[16:]:
+        load.wait()
+    for copy in mine + shares:
+        copy.wait_recv()
     lhs1 = L1[...]
-    places = {}
-    for j in FAR:
-        for k in range(4):
-            index = ((x + j) % NX) * NZ + (z + FAR[k]) % NZ
-            places[j, k] = pl.ds(pl.multiple_of(index * 256, 256), 256)
-            PM[j, k] = nt(lhs1, WM[places[j, k], :])
-    loads[17].wait()
-    loads[18].wait()
-    for copy in mine:
-        copy.wait_recv()
-    swap.wait_recv()
-    L2[:, 0:128] = (own_state + AR[...].astype(F32)).astype(BF16)
     lhs2 = L2[...]
     first_core = c == 0
     to_mate = {}
-    for k in range(4):
-        for j in FAR:
-            part = PM[j, k] + nn(lhs2, WS[:, places[j, k]])
-            lower, upper_half = part[:, 0:128], part[:, 128:256]
-            Q[j, k] = jnp.where(first_core, lower, upper_half)
-            PS[j, k] = jnp.where(first_core, upper_half, lower).astype(BF16)
-            to_mate[j, k] = go(remote(PS.at[j, k], PR.at[j, k], mate))
+
+    def input_block(j, k):
+        index = ((x + j) % NX) * NZ + (z + FAR[k]) % NZ
+        at = pl.ds(pl.multiple_of(index * 256, 256), 256)
+        part = nt(lhs1, WM[at, :]) + nn(lhs2, WS[:, at])
+        lower, upper_half = part[:, 0:128], part[:, 128:256]
+        Q[j, k] = jnp.where(first_core, lower, upper_half)
+        PS[j, k] = jnp.where(first_core, upper_half, lower).astype(BF16)
+        to_mate[j, k] = go(remote(PS.at[j, k], PR.at[j, k], mate))
 
     arrived = set()
 
@@ -375,9 +415,13 @@
         else:
             totals[h] = value
 
-    for h in range(H):
-        for k in range(4):
-            send_x(h, k)
+    for k in range(5):
+        if k < 4:
+            for j in FAR:
+                input_block(j, k)
+        if k > 0:
+            for h in range(H):
+                send_x(h, k - 1)
     for h in range(H):
         for k in range(4):
             send_z(h, k)
@@ -397,11 +441,16 @@
     for copies in first:
         for copy in copies:
             copy.wait_send()
-    for copy in pending:
+    for copy in pending + shares:
         copy.wait_send()
 
-
-N_COPIES = H * (4 + 12 + 16 + 12 + 3) + 2 + 1 + 16
+    @pl.when(inner)
+    def _():
+        for copy in swaps + passes:
+            copy.wait_send()
+
+
+N_COPIES = H * (4 + 12 + 16 + 12 + 3) + 16 + 16
 
 
 def body(
@@ -430,7 +479,7 @@
         scratch_shapes=[
             pltpu.VMEM((4096, 512), BF16),
             pltpu.VMEM((16, 256, 256), BF16),
-            pltpu.VMEM((256, 4096), BF16),
+            pltpu.VMEM((384, 4096), BF16),
             pltpu.VMEM((2, 4, 4) + block, BF16),
             pltpu.VMEM((4, 4) + block, F32),
             pltpu.VMEM((4, 4) + block, BF16),
@@ -454,11 +503,8 @@
             pltpu.VMEM(block, F32),
             pltpu.VMEM((8, 256), F32),
             pltpu.VMEM((T, 512), BF16),
-            pltpu.VMEM((T, 256), BF16),
-            pltpu.VMEM(block, BF16),
-            pltpu.VMEM(block, BF16),
-            pltpu.VMEM((4, 4, T, 256), F32),
-            pltpu.SemaphoreType.DMA((20,)),
+            pltpu.VMEM((T, 384), BF16),
+            pltpu.SemaphoreType.DMA((21,)),
             pltpu.SemaphoreType.DMA((N_COPIES,)),
             pltpu.SemaphoreType.DMA((N_COPIES,)),
         ],

time: 144 us -> 137 us (0.951); the launches traced: 142 us -> 137 us
  Pallas kernels: 133 us -> 128 us
    pallas_call x1, Pallas kernels: 133 us -> 128 us  [body(): pl.pallas_call(kernel, out_shape=jax.ShapeDtypeStruct((T, T), BF16), in_s...]
where the time goes in v3:
time: 137 us
  Pallas kernels  128 us (93%)
  local copies, waits for them, and re-layouts  8.23 us (6%)
    pallas_call x1, Pallas kernels, body(): pl.pallas_call(kernel, out_shape=jax.ShapeDtypeStruct((T, T), BF16), in_s...  128 us
    unnamed x21, local copies, waits for them, and re-layouts  8.17 us

profile of v3, /device:TPU:1, one launch (start us, length us, event | category | flops | bytes accessed | tf_op | source)
XLA Modules:
  0.0 137.1 jit_solution(11460273661764048295)
XLA Ops:
  0.0 0.0 copy-start
  0.0 0.7 dynamic-slice_bitcast_fusion
  0.8 0.7 select_maximum_fusion.vec_ref
  1.5 0.8 copy.15
  2.3 0.0 copy-done
  2.3 0.1 constant_dynamic-slice_fusion
  2.4 0.9 copy.17
  3.3 0.0 copy-start.1
  3.3 0.0 copy-start.2
  3.3 0.0 copy-start.3
  3.3 0.0 copy-start.4
  3.3 0.0 copy-start.5
  3.4 0.0 copy-start.6
  3.4 5.0 %copy.16 = bf16[512,8,2,256]{3,1,2,0:T(8,128)(2,1)} copy(bf16[512,8,2,256]{3,2,1,0:T(2,128)(2,1)} %bitcast.36) | data formatting | bytes 8388608
  8.4 0.0 copy-done.1
  8.4 0.0 copy-done.2
  8.4 0.0 copy-done.3
  8.4 0.0 copy-done.4
  8.4 0.0 copy-done.5
  8.4 0.0 copy-done.6
  8.4 128.1 %relay.1 = bf16[128,128]{1,0:T(8,128)(2,1)S(1)} custom-call(bf16[4096,512]{1,0:T(8,128)(2,1)} %bitcast.35, bf16[2,32,4096]{2,1,0:T(8,128)(2,1)S(1)} %bitcast.29, bf16[256,4096]{1,0:T(8,128)(2,1)S(1)} %bitcast.27, bf16[4,4096]{1,0:T(4,128)(2,1)S(1)} %bitcast.32, bf16[128,512]{1,0:T(8,128)(2,1)S(1)} %bitcast.28, bf16[128,256]{1,0:T(8,128)(2,1)S(1)} %bitcast.30, ...), custom_call_target="tpu_custom_call" | custom-call | tf_op jit(solution)/shard_map/relay/pallas_call | solution.py:474
  136.5 0.6 copy.25
  (3 shorter events, 0.0 us)
Async XLA Ops:
  0.0 2.3 %copy-start = (bf16[1,128,2,1024]{3,2,1,0:T(2,128)(2,1)S(1)}, bf16[1,128,2,1024]{3,2,1,0:T(2,128)(2,1)}, u32[]{:S(2)}) copy-start(bf16[1,128,2,1024]{3,2,1,0:T(2,128)(2,1)} %param.25) | copy-start | bytes 1572868
  3.3 5.1 %copy-start.1 = (bf16[1,256,4096]{2,1,0:T(8,128)(2,1)S(1)}, bf16[1,256,4096]{2,1,0:T(8,128)(2,1)}, u32[]{:S(2)}) copy-start(bf16[1,256,4096]{2,1,0:T(8,128)(2,1)} %param.17) | copy-start | bytes 6291460
  3.3 5.1 %copy-start.2 = (bf16[1,4096,2,32]{1,3,2,0:T(8,128)(2,1)S(1)}, bf16[1,4096,2,32]{1,3,2,0:T(8,128)(2,1)}, u32[]{:S(2)}) copy-start(bf16[1,4096,2,32]{1,3,2,0:T(8,128)(2,1)} %param.15) | copy-start | bytes 1572868
  3.3 5.1 %copy-start.3 = (bf16[1,4,4096]{2,1,0:T(4,128)(2,1)S(1)}, bf16[1,4,4096]{2,1,0:T(4,128)(2,1)}, u32[]{:S(2)}) copy-start(bf16[1,4,4096]{2,1,0:T(4,128)(2,1)} %param.16) | copy-start | bytes 98308
  3.3 5.1 %copy-start.4 = (bf16[128,128]{1,0:T(8,128)(2,1)S(1)}, bf16[128,128]{1,0:T(8,128)(2,1)}, u32[]{:S(2)}) copy-start(bf16[128,128]{1,0:T(8,128)(2,1)} %og_ref.1) | copy-start | bytes 98308
  3.3 5.1 %copy-start.5 = (f32[1,4,256]{2,1,0:T(4,128)S(1)}, f32[1,4,256]{2,1,0:T(4,128)}, u32[]{:S(2)}) copy-start(f32[1,4,256]{2,1,0:T(4,128)} %param.18) | copy-start | bytes 12292
  3.4 5.1 %copy-start.6 = (f32[1,256]{1,0:T(1,128)S(1)}, f32[1,256]{1,0:T(1,128)}, u32[]{:S(2)}) copy-start(f32[1,256]{1,0:T(1,128)} %gain_ref.1) | copy-start | bytes 3076

commit v4 on v3

--- a/solution.py
+++ b/solution.py
@@ -58,10 +58,12 @@
 
 def kernel(
     wm_hbm, ws_hbm, wo_hbm,
-    wt_ref, main_ref, state_ref, stepin_ref, vec_ref, cm_ref, cs_ref, gain_ref, og_ref,
+    bias_hbm, decay_hbm, skip_hbm,
+    wt_hbm, main_hbm, state_hbm, stepin_hbm, cm_hbm, cs_hbm, gain_hbm, og_hbm,
     out_ref,
-    WM, WO, WS, G, Q, PS, PR, XS, XR, ZS, ZR,
-    NRM, SGI, YSP, MIX, STL, DSM, DSS, EM, SC, WTC, SCM, BC, SIG, SK, L1, L2,
+    bias_ref, decay_ref, skip_ref, wt_ref, main_ref, state_ref, stepin_ref, cm_ref, cs_ref, gain_ref,
+    RAW, W, WO, STEP, G, Q, PS, PR, XS, XR, ZS, ZR,
+    NRM, SGI, YSP, MIX, STL, DSM, DSS, EM, SC, WTC, SCM, BC, SIG, SK, CS, L,
     wsem, ssem, rsem,
 ):
     s = lax.axis_index("pipe")
@@ -118,16 +120,25 @@
     for p in partners:
         pl.semaphore_signal(barrier, inc=1, device_id=p, device_id_type=MESH)
 
+    group = pl.ds(pl.multiple_of(t // 4 * 128, 128), 128)
+    small = [
+        (main_hbm, main_ref), (state_hbm.at[:, :, group], state_ref), (cm_hbm, cm_ref),
+        (cs_hbm.at[:, :, group], cs_ref), (stepin_hbm, stepin_ref), (bias_hbm, bias_ref),
+        (decay_hbm, decay_ref), (skip_hbm, skip_ref), (gain_hbm, gain_ref), (wt_hbm, wt_ref),
+    ]
+    small = [pltpu.make_async_copy(src, dst, wsem.at[21 + i]) for i, (src, dst) in enumerate(small)]
+    for load in small:
+        load.start()
     loads = [
         pltpu.make_async_copy(wo_hbm.at[:, pl.ds(i * 256, 256)], WO.at[i], wsem.at[i])
         for i in range(16)
     ]
-    loads.append(pltpu.make_async_copy(wm_hbm, WM, wsem.at[16]))
+    loads.append(pltpu.make_async_copy(wm_hbm, RAW, wsem.at[16]))
     m = t % 4
     cuts = [(half, pl.ds(part * 2048, 2048)) for half in range(2) for part in range(2)]
 
     def columns(member, half, lanes):
-        return WS.at[pl.ds(pl.multiple_of(half * 128 + member * 32, 32), 32), lanes]
+        return W.at[pl.ds(pl.multiple_of(512 + half * 128 + member * 32, 32), 32), lanes]
 
     def own_columns(half, lanes):
         return ws_hbm.at[half, :, lanes]
@@ -158,7 +169,7 @@
             )
         return copies
 
-    first = [hand_off(og_ref, h) for h in range(H)]
+    first = [hand_off(og_hbm, h) for h in range(H)]
 
     @pl.when(s == 0)
     def _():
@@ -189,8 +200,27 @@
             shares[q].start()
 
     early = s != 3
-    WS[256:384, :] = jnp.zeros((128, 4096), BF16)
-    WS[256:260, :] = wt_ref[...]
+    for load in small:
+        load.wait()
+    W[768:896, :] = jnp.zeros((128, 4096), BF16)
+    W[768:772, :] = wt_ref[...]
+
+    apart_row = lax.broadcasted_iota(jnp.int32, (256, 256), 0)
+    apart_col = lax.broadcasted_iota(jnp.int32, (256, 256), 1)
+    apart = (apart_col == 2 * (apart_row % 128) + apart_row // 128).astype(BF16)
+
+    def turn(first_block, last_block):
+        def one(i, carry):
+            at = pl.ds(pl.multiple_of(i * 128, 128), 128)
+            both = lax.dot_general(
+                RAW[at].reshape(256, 256), apart, (((0,), (1,)), ((), ())),
+                preferred_element_type=F32,
+            ).astype(BF16)
+            W[0:256, at] = both[:, 0:128]
+            W[256:512, at] = both[:, 128:256]
+            return carry
+
+        lax.fori_loop(first_block, last_block, one, 0, unroll=4)
 
     rows = lax.broadcasted_iota(jnp.int32, (T, 256), 0)
     ri = lax.broadcasted_iota(jnp.int32, (T, T), 0)
@@ -200,32 +230,46 @@
         lax.broadcasted_iota(jnp.int32, (T, 256), 0)
         == lax.broadcasted_iota(jnp.int32, (T, 256), 1) // 64
     ).astype(F32)
-    gate = main_ref[:, 0:256].astype(F32)
+    pair_in = nn(apart, main_ref[...].reshape(256, 256))
+    gate = pair_in[0:128]
     cm = cm_ref[...]
-    cs = cs_ref[...]
-    mixed = conv(main_ref[:, 256:512].astype(F32), cm, rows)
+    cs = jnp.concatenate([cs_ref[:, 0, :], cs_ref[:, 1, :]], axis=1)
+    CS[...] = cs
+    mixed = conv(pair_in[128:256], cm, rows)
     sig = jax.nn.sigmoid(mixed)
     mix = mixed * sig
     DSM[...] = sig * (1.0 + mixed * (1.0 - sig))
     MIX[...] = mix
-    states = conv(state_ref[...].astype(F32), cs, rows)
+    pair_in = nn(apart, state_ref[...].reshape(256, 128))
+    states = conv(jnp.concatenate([pair_in[0:128], pair_in[128:256]], axis=1), cs, rows)
     sig = jax.nn.sigmoid(states)
     DSS[...] = sig * (1.0 + states * (1.0 - sig))
     states = states * sig
     BC[...] = states.astype(BF16)
     scores = nt(states[:, 128:256], states[:, 0:128], HIGHEST)
     SC[...] = scores
-    vec = vec_ref[...]
-    raw = stepin_ref[...] + vec[0:1]
+    heads = lax.broadcasted_iota(jnp.int32, (1, T), 1)
+    channels = lax.broadcasted_iota(jnp.int32, (1, 256), 1) // 64
+
+    def by_lane(ref, lanes):
+        out = jnp.zeros(lanes.shape, F32)
+        for h in range(4):
+            out = jnp.where(lanes == h, ref[0, h], out)
+        return out
+
+    STEP[...] = jnp.zeros((T, T), F32)
+    STEP[0:4, :] = stepin_ref[...].astype(F32)
+    raw = STEP[...].T + by_lane(bias_ref, heads)
     SIG[...] = jax.nn.sigmoid(raw)
     step = jnp.maximum(raw, 0.0) + jnp.log1p(jnp.exp(-jnp.abs(raw)))
-    rate = -jnp.exp(vec[1:2])
+    rate = -jnp.exp(by_lane(decay_ref, heads))
+    SK[0:1, 0:128] = rate
     run_col = nn(causal.astype(F32), step * rate, HIGHEST)
     run_row = run_col.T
     stepl = nn(step, rep, HIGHEST)
     STL[...] = stepl
-    SK[...] = nn(vec, rep, HIGHEST)
-    skipl = SK[2:3]
+    skipl = by_lane(skip_ref, channels)
+    SK[1:2] = skipl
     scaled = mix * stepl
     low = ci < 64
     ys = []
@@ -265,6 +309,12 @@
     to_o = {hk: spread(0, 2, to_opposite, *hk) for hk in grid}
     to_m = {(j, h, k): spread(j, j, mate, h, k) for j in range(4) for h, k in grid}
 
+    loads[16].wait()
+
+    @pl.when(early)
+    def _():
+        turn(0, 32)
+
     @pl.when(jnp.logical_and(early, inner))
     def _():
         relay(range(4))
@@ -284,15 +334,29 @@
     def _():
         relay((0, 1))
 
-    for h, k in grid:
+    @pl.when(s == 3)
+    def _():
+        turn(0, 24)
+
+    for n, (h, k) in enumerate(grid):
         to_r[h, k].wait_recv()
         go(to_m[3, h, k])
         to_l[h, k].wait_recv()
         go(to_m[1, h, k])
+        if n == 2 * H - 1:
+
+            @pl.when(jnp.logical_and(s == 3, inner))
+            def _():
+                relay((2,))
+
 
     @pl.when(jnp.logical_and(s == 3, inner))
     def _():
-        relay((2, 3))
+        relay((3,))
+
+    @pl.when(s == 3)
+    def _():
+        turn(24, 32)
 
     for i in range(16):
         loads[i].wait()
@@ -321,7 +385,7 @@
     mu = jnp.sum(dn * nrm, axis=1, keepdims=True) * (1.0 / 256.0)
     e = dn - nrm * mu
     dy = e * SGI[...]
-    L1[:, 0:256] = (e * YSP[...]).astype(BF16)
+    L[:, 0:256] = (e * YSP[...]).astype(BF16)
     dyb = dy.astype(BF16)
     ds = None
     masks = []
@@ -332,7 +396,7 @@
     db = nn(ds.T.astype(BF16), BC[:, 128:256])
     dc = nn(ds.astype(BF16), BC[:, 0:128])
     dstate = jnp.concatenate([db, dc], axis=1) * DSS[...]
-    L2[:, 0:256] = conv_back(dstate, cs_ref[...], rows).astype(BF16)
+    L[:, 512:768] = conv_back(dstate, CS[...], rows).astype(BF16)
     dscs = []
     for pair in range(2):
         dyp = dyb[:, pair * 128 : pair * 128 + 128]
@@ -340,8 +404,8 @@
         both = jnp.concatenate([jnp.where(low, dyp, zero), jnp.where(low, zero, dyp)], axis=0)
         dscs.append(nn(WTC[pair], both))
     dscaled = jnp.concatenate(dscs, axis=1)
-    dmix = (dscaled * STL[...] + SK[2:3] * dy) * DSM[...]
-    L1[:, 256:512] = conv_back(dmix, cm_ref[...], rows).astype(BF16)
+    dmix = (dscaled * STL[...] + SK[1:2] * dy) * DSM[...]
+    L[:, 256:512] = conv_back(dmix, cm_ref[...], rows).astype(BF16)
     upper = (ci >= ri).astype(BF16)
     sums = nn(upper, jnp.concatenate(masks, axis=1))
     before = jnp.concatenate([ci < ri] * 4, axis=1)
@@ -356,26 +420,25 @@
         == lax.broadcasted_iota(jnp.int32, (256, T), 1)
     ).astype(BF16)
     dstep = nn((dscaled * MIX[...]).astype(BF16), pick64)
-    dstep = dstep + ddecay * -jnp.exp(vec_ref[1:2])
-    L2[:, 256:384] = (dstep * SIG[...]).astype(BF16)
+    dstep = dstep + ddecay * SK[0:1, 0:128]
+    L[:, 768:896] = (dstep * SIG[...]).astype(BF16)
 
     @pl.when(jnp.logical_and(s == 3, jnp.logical_not(inner)))
     def _():
         accept()
 
-    for load in loads[16:]:
+    for load in loads[17:]:
         load.wait()
     for copy in mine + shares:
         copy.wait_recv()
-    lhs1 = L1[...]
-    lhs2 = L2[...]
+    lhs = L[...]
     first_core = c == 0
     to_mate = {}
 
     def input_block(j, k):
         index = ((x + j) % NX) * NZ + (z + FAR[k]) % NZ
         at = pl.ds(pl.multiple_of(index * 256, 256), 256)
-        part = nt(lhs1, WM[at, :]) + nn(lhs2, WS[:, at])
+        part = nn(lhs, W[:, at])
         lower, upper_half = part[:, 0:128], part[:, 128:256]
         Q[j, k] = jnp.where(first_core, lower, upper_half)
         PS[j, k] = jnp.where(first_core, upper_half, lower).astype(BF16)
@@ -457,29 +520,31 @@
     weight_main, weight_state, weight_step, weight_out, conv_main, conv_state, step_bias,
     decay_log, skip_gain, norm_gain, saved_main, saved_state, saved_step, output_grad,
 ):
-    group = lax.axis_index("tensor") // 4
-    wm = weight_main[0].reshape(4096, 512)
     ws = jnp.transpose(weight_state[0], (1, 2, 0))
-    main = saved_main[0].reshape(T, 512)
-    state = lax.dynamic_slice_in_dim(saved_state[0], group * 128, 128, 2).reshape(T, 256)
-    cs = lax.dynamic_slice_in_dim(conv_state[0], group * 128, 128, 2).reshape(4, 256)
-    stepin = jnp.pad(saved_step[0].astype(F32).T, ((0, 0), (0, 124)))
-    vec = jnp.pad(
-        jnp.concatenate([step_bias, decay_log, skip_gain], axis=0), ((0, 5), (0, 124))
-    )
     vmem = pl.BlockSpec(memory_space=pltpu.VMEM)
-    hbm = pl.BlockSpec(memory_space=pl.ANY)
+    hbm = pl.BlockSpec(memory_space=pltpu.HBM)
     block = (T, T)
     wide = (T, 256)
     result = pl.pallas_call(
         kernel,
         out_shape=jax.ShapeDtypeStruct((T, T), BF16),
-        in_specs=[hbm] * 3 + [vmem] * 9,
+        in_specs=[hbm] * 14,
         out_specs=vmem,
         scratch_shapes=[
-            pltpu.VMEM((4096, 512), BF16),
+            pltpu.SMEM((1, 4), F32),
+            pltpu.SMEM((1, 4), F32),
+            pltpu.SMEM((1, 4), F32),
+            pltpu.VMEM((4, 4096), BF16),
+            pltpu.VMEM((T, 2, 256), BF16),
+            pltpu.VMEM((T, 2, 128), BF16),
+            pltpu.VMEM((4, T), BF16),
+            pltpu.VMEM((4, 256), F32),
+            pltpu.VMEM((4, 2, 128), F32),
+            pltpu.VMEM((1, 256), F32),
+            pltpu.VMEM((4096, 2, 256), BF16),
+            pltpu.VMEM((896, 4096), BF16),
             pltpu.VMEM((16, 256, 256), BF16),
-            pltpu.VMEM((384, 4096), BF16),
+            pltpu.VMEM(block, F32),
             pltpu.VMEM((2, 4, 4) + block, BF16),
             pltpu.VMEM((4, 4) + block, F32),
             pltpu.VMEM((4, 4) + block, BF16),
@@ -502,17 +567,21 @@
             pltpu.VMEM(wide, BF16),
             pltpu.VMEM(block, F32),
             pltpu.VMEM((8, 256), F32),
-            pltpu.VMEM((T, 512), BF16),
-            pltpu.VMEM((T, 384), BF16),
-            pltpu.SemaphoreType.DMA((21,)),
+            pltpu.VMEM((4, 256), F32),
+            pltpu.VMEM((T, 896), BF16),
+            pltpu.SemaphoreType.DMA((31,)),
             pltpu.SemaphoreType.DMA((N_COPIES,)),
             pltpu.SemaphoreType.DMA((N_COPIES,)),
         ],
         compiler_params=pltpu.CompilerParams(
-            collective_id=0, has_side_effects=True, vmem_limit_bytes=48 * 1024 * 1024
+            collective_id=0, has_side_effects=True, vmem_limit_bytes=67043328
         ),
         name="relay",
-    )(wm, ws, weight_out[0], weight_step[0], main, state, stepin, vec, conv_main[0], cs, norm_gain, output_grad)
+    )(
+        weight_main[0], ws, weight_out[0], step_bias, decay_log, skip_gain, weight_step[0],
+        saved_main[0], saved_state[0], saved_step[0], conv_main[0], conv_state[0], norm_gain,
+        output_grad,
+    )
     return result[None]
 
 

time: 137 us -> 127 us (0.927)
  local copies, waits for them, and re-layouts: 8.23 us -> 1.38 us
  Pallas kernels: 128 us -> 126 us
    unnamed x21 -> x1, local copies, waits for them, and re-layouts: 8.17 us -> 1.38 us
    pallas_call x1, Pallas kernels: 128 us -> 126 us  [body(): pl.pallas_call(kernel, out_shape=jax.ShapeDtypeStruct((T, T), BF16), in_s...]
where the time goes in v4:
time: 127 us
  Pallas kernels  126 us (99%)
  local copies, waits for them, and re-layouts  1.38 us (1%)
    pallas_call x1, Pallas kernels, body(): pl.pallas_call(kernel, out_shape=jax.ShapeDtypeStruct((T, T), BF16), in_s...  126 us

profile of v4, /device:TPU:1, one launch (start us, length us, event | category | flops | bytes accessed | tf_op | source)
XLA Modules:
  0.0 127.0 jit_solution(10630409191451339797)
XLA Ops:
  0.0 125.6 %relay.1 = bf16[128,128]{1,0:T(8,128)(2,1)} custom-call(bf16[4096,2,256]{2,1,0:T(2,128)(2,1)} %bitcast.12, bf16[2,32,4096]{2,1,0:T(8,128)(2,1)} %bitcast.14, bf16[256,4096]{1,0:T(8,128)(2,1)} %bitcast.13, f32[1,4]{1,0:T(1,128)} %bias_hbm.1, f32[1,4]{1,0:T(1,128)} %decay_hbm.1, f32[1,4]{1,0:T(1,128)} %skip_hbm.1, bf16[4,4096]{1,0:T(4,128)(2,1)} %bitcast.18, ...), custom_call_target="tpu_custom_call" | custom-call | tf_op jit(solution)/shard_map/relay/pallas_call | solution.py:528
  125.6 1.4 %copy.16 = bf16[1,128,128]{2,1,0:T(8,128)(2,1)} copy(bf16[1,128,128]{2,1,0:T(8,128)(2,1)} %bitcast.17) | data formatting | bytes 65536

commit v5 on v4

--- a/solution.py
+++ b/solution.py
@@ -63,7 +63,7 @@
     out_ref,
     bias_ref, decay_ref, skip_ref, wt_ref, main_ref, state_ref, stepin_ref, cm_ref, cs_ref, gain_ref,
     RAW, W, WO, STEP, G, Q, PS, PR, XS, XR, ZS, ZR,
-    NRM, SGI, YSP, MIX, STL, DSM, DSS, EM, SC, WTC, SCM, BC, SIG, SK, CS, L,
+    NRM, SGI, YSP, MIX, STL, DSM, DSS, EM, SC, WTC, SCM, BC, SIG, SK, CS, L, ACC,
     wsem, ssem, rsem,
 ):
     s = lax.axis_index("pipe")
@@ -162,7 +162,7 @@
             i = hand_ids[4 * h + n]
             copies.append(
                 pltpu.make_async_remote_copy(
-                    src_ref=block.at[pieces[h]], dst_ref=G.at[c, 0, (4 - o) % 4, pieces[h]],
+                    src_ref=block.at[pieces[h]], dst_ref=G.at[c, (4 - o) % 4, 0, pieces[h]],
                     send_sem=ssem.at[i], recv_sem=rsem.at[i],
                     device_id=dev(place(x, (z + o) % NZ, c), below), device_id_type=MESH,
                 )
@@ -301,13 +301,15 @@
     ks = (0, 1, 3, 2)
 
     def spread(src_j, dst_j, target, h, k):
-        return remote(G.at[c, src_j, k, pieces[h]], G.at[c, dst_j, k, pieces[h]], target)
+        return remote(G.at[c, k, src_j, pieces[h]], G.at[c, k, dst_j, pieces[h]], target)
 
     grid = [(h, k) for h in range(H) for k in ks]
     to_r = {hk: spread(0, 3, to_right, *hk) for hk in grid}
     to_l = {hk: spread(0, 1, to_left, *hk) for hk in grid}
     to_o = {hk: spread(0, 2, to_opposite, *hk) for hk in grid}
-    to_m = {(j, h, k): spread(j, j, mate, h, k) for j in range(4) for h, k in grid}
+    to_m = {
+        (h, k): remote(G.at[c, k, :, pieces[h]], G.at[c, k, :, pieces[h]], mate) for h, k in grid
+    }
 
     loads[16].wait()
 
@@ -328,7 +330,6 @@
         go(to_o[h, k])
         go(to_r[h, k])
         go(to_l[h, k])
-        go(to_m[0, h, k])
 
     @pl.when(jnp.logical_and(s == 3, inner))
     def _():
@@ -338,47 +339,43 @@
     def _():
         turn(0, 24)
 
+    for i in range(16):
+        loads[i].wait()
+
+    def multiply(k):
+        lefts, rights = [], []
+        for h in range(H):
+            to_m[h, k].wait_recv()
+        for j in range(4):
+            lefts += [G[0, k, j], G[1, k, j]]
+            rights.append(WO[((x + j) % NX) * NZ + (z + k) % NZ])
+        part = nt(jnp.concatenate(lefts, axis=1), jnp.concatenate(rights, axis=1))
+        return part if k == ks[0] else ACC[...] + part
+
     for n, (h, k) in enumerate(grid):
+        to_o[h, k].wait_recv()
         to_r[h, k].wait_recv()
-        go(to_m[3, h, k])
         to_l[h, k].wait_recv()
-        go(to_m[1, h, k])
+        go(to_m[h, k])
         if n == 2 * H - 1:
 
             @pl.when(jnp.logical_and(s == 3, inner))
             def _():
                 relay((2,))
 
+        if h == H - 1 and k != ks[0]:
+            before = ks[ks.index(k) - 1]
+            ACC[...] = multiply(before)
+
+    @pl.when(s == 3)
+    def _():
+        turn(24, 32)
 
     @pl.when(jnp.logical_and(s == 3, inner))
     def _():
         relay((3,))
 
-    @pl.when(s == 3)
-    def _():
-        turn(24, 32)
-
-    for i in range(16):
-        loads[i].wait()
-    totals = [None]
-
-    def multiply(j):
-        for k in ks:
-            for h in range(H):
-                to_m[j, h, k].wait_recv()
-            index = ((x + j) % NX) * NZ + (z + k) % NZ
-            block = jnp.concatenate([G[0, j, k], G[1, j, k]], axis=1)
-            part = nt(block, WO[index])
-            totals[0] = part if totals[0] is None else totals[0] + part
-
-    multiply(0)
-    multiply(3)
-    for h, k in grid:
-        to_o[h, k].wait_recv()
-        go(to_m[2, h, k])
-    multiply(1)
-    multiply(2)
-    acc = totals[0]
+    acc = multiply(ks[3])
 
     dn = acc * gain_ref[...]
     nrm = NRM[...]
@@ -441,16 +438,15 @@
         part = nn(lhs, W[:, at])
         lower, upper_half = part[:, 0:128], part[:, 128:256]
         Q[j, k] = jnp.where(first_core, lower, upper_half)
-        PS[j, k] = jnp.where(first_core, upper_half, lower).astype(BF16)
-        to_mate[j, k] = go(remote(PS.at[j, k], PR.at[j, k], mate))
+        PS[k, j] = jnp.where(first_core, upper_half, lower).astype(BF16)
 
     arrived = set()
 
     def chip_sum(j, k, h):
-        if (j, k) not in arrived:
-            arrived.add((j, k))
-            to_mate[j, k].wait_recv()
-        return Q[j, k, pieces[h]] + PR[j, k, pieces[h]].astype(F32)
+        if k not in arrived:
+            arrived.add(k)
+            to_mate[k].wait_recv()
+        return Q[j, k, pieces[h]] + PR[k, j, pieces[h]].astype(F32)
 
     sends = {}
     zcopies = {}
@@ -482,6 +478,7 @@
         if k < 4:
             for j in FAR:
                 input_block(j, k)
+            to_mate[k] = go(remote(PS.at[k], PR.at[k], mate))
         if k > 0:
             for h in range(H):
                 send_x(h, k - 1)
@@ -513,7 +510,7 @@
             copy.wait_send()
 
 
-N_COPIES = H * (4 + 12 + 16 + 12 + 3) + 16 + 16
+N_COPIES = H * (4 + 12 + 4 + 12 + 3) + 4 + 16
 
 
 def body(
@@ -569,6 +566,7 @@
             pltpu.VMEM((8, 256), F32),
             pltpu.VMEM((4, 256), F32),
             pltpu.VMEM((T, 896), BF16),
+            pltpu.VMEM(wide, F32),
             pltpu.SemaphoreType.DMA((31,)),
             pltpu.SemaphoreType.DMA((N_COPIES,)),
             pltpu.SemaphoreType.DMA((N_COPIES,)),

time: 127 us -> 125 us (0.984)
  Pallas kernels: 126 us -> 123 us
    pallas_call x1, Pallas kernels: 126 us -> 123 us  [body(): pl.pallas_call(kernel, out_shape=jax.ShapeDtypeStruct((T, T), BF16), in_s...]
where the time goes in v5:
time: 125 us; the launch traced here: 124 us
  Pallas kernels  123 us (98%)
  local copies, waits for them, and re-layouts  1.38 us (1%)
    pallas_call x1, Pallas kernels, body(): pl.pallas_call(kernel, out_shape=jax.ShapeDtypeStruct((T, T), BF16), in_s...  123 us

profile of v5, /device:TPU:1, one launch (start us, length us, event | category | flops | bytes accessed | tf_op | source)
XLA Modules:
  0.0 124.4 jit_solution(17176840348423845570)
XLA Ops:
  0.0 123.0 %relay.1 = bf16[128,128]{1,0:T(8,128)(2,1)} custom-call(bf16[4096,2,256]{2,1,0:T(2,128)(2,1)} %bitcast.12, bf16[2,32,4096]{2,1,0:T(8,128)(2,1)} %bitcast.14, bf16[256,4096]{1,0:T(8,128)(2,1)} %bitcast.13, f32[1,4]{1,0:T(1,128)} %bias_hbm.1, f32[1,4]{1,0:T(1,128)} %decay_hbm.1, f32[1,4]{1,0:T(1,128)} %skip_hbm.1, bf16[4,4096]{1,0:T(4,128)(2,1)} %bitcast.18, ...), custom_call_target="tpu_custom_call" | custom-call | tf_op jit(solution)/shard_map/relay/pallas_call | solution.py:525
  123.0 1.4 %copy.16 = bf16[1,128,128]{2,1,0:T(8,128)(2,1)} copy(bf16[1,128,128]{2,1,0:T(8,128)(2,1)} %bitcast.17) | data formatting | bytes 65536

commit v6 on v5

--- a/solution.py
+++ b/solution.py
@@ -14,7 +14,7 @@
 NZ = 4
 T = 128
 FAR = (2, 1, 3, 0)
-H = 1
+H = 2
 TH = T // H
 
 
@@ -480,8 +480,10 @@
                 input_block(j, k)
             to_mate[k] = go(remote(PS.at[k], PR.at[k], mate))
         if k > 0:
-            for h in range(H):
-                send_x(h, k - 1)
+            send_x(0, k - 1)
+    for h in range(1, H):
+        for k in range(4):
+            send_x(h, k)
     for h in range(H):
         for k in range(4):
             send_z(h, k)

time: 125 us -> 121 us (0.968)
  Pallas kernels: 123 us -> 120 us
    pallas_call x1, Pallas kernels: 123 us -> 120 us  [body(): pl.pallas_call(kernel, out_shape=jax.ShapeDtypeStruct((T, T), BF16), in_s...]
where the time goes in v6:
time: 121 us
  Pallas kernels  120 us (99%)
  local copies, waits for them, and re-layouts  1.38 us (1%)
    pallas_call x1, Pallas kernels, body(): pl.pallas_call(kernel, out_shape=jax.ShapeDtypeStruct((T, T), BF16), in_s...  120 us

profile of v6, /device:TPU:1, one launch (start us, length us, event | category | flops | bytes accessed | tf_op | source)
XLA Modules:
  0.0 121.2 jit_solution(6522694082576649398)
XLA Ops:
  0.0 119.9 %relay.1 = bf16[128,128]{1,0:T(8,128)(2,1)} custom-call(bf16[4096,2,256]{2,1,0:T(2,128)(2,1)} %bitcast.12, bf16[2,32,4096]{2,1,0:T(8,128)(2,1)} %bitcast.14, bf16[256,4096]{1,0:T(8,128)(2,1)} %bitcast.13, f32[1,4]{1,0:T(1,128)} %bias_hbm.1, f32[1,4]{1,0:T(1,128)} %decay_hbm.1, f32[1,4]{1,0:T(1,128)} %skip_hbm.1, bf16[4,4096]{1,0:T(4,128)(2,1)} %bitcast.18, ...), custom_call_target="tpu_custom_call" | custom-call | tf_op jit(solution)/shard_map/relay/pallas_call | solution.py:527
  119.9 1.4 %copy.16 = bf16[1,128,128]{2,1,0:T(8,128)(2,1)} copy(bf16[1,128,128]{2,1,0:T(8,128)(2,1)} %bitcast.17) | data formatting | bytes 65536

commit v7 on v6

--- a/solution.py
+++ b/solution.py
@@ -194,8 +194,8 @@
             passes[q].start()
             shares[q].start()
 
-    def accept():
-        for q in range(4):
+    def accept(chosen):
+        for q in chosen:
             passes[q].wait_recv()
             shares[q].start()
 
@@ -323,7 +323,7 @@
 
     @pl.when(jnp.logical_and(early, jnp.logical_not(inner)))
     def _():
-        accept()
+        accept(range(4))
 
     for h, k in grid:
         first[h][FAR.index((4 - k) % 4)].wait_recv()
@@ -357,11 +357,11 @@
         to_r[h, k].wait_recv()
         to_l[h, k].wait_recv()
         go(to_m[h, k])
-        if n == 2 * H - 1:
+        if n in (1, 5):
 
             @pl.when(jnp.logical_and(s == 3, inner))
             def _():
-                relay((2,))
+                relay((2,) if n == 1 else (3,))
 
         if h == H - 1 and k != ks[0]:
             before = ks[ks.index(k) - 1]
@@ -371,9 +371,9 @@
     def _():
         turn(24, 32)
 
-    @pl.when(jnp.logical_and(s == 3, inner))
-    def _():
-        relay((3,))
+    @pl.when(jnp.logical_and(s == 3, jnp.logical_not(inner)))
+    def _():
+        accept((0, 1))
 
     acc = multiply(ks[3])
 
@@ -422,7 +422,7 @@
 
     @pl.when(jnp.logical_and(s == 3, jnp.logical_not(inner)))
     def _():
-        accept()
+        accept((2, 3))
 
     for load in loads[17:]:
         load.wait()

time: 121 us -> 121 us (level)
  no operation moved by 1% of the time
where the time goes in v7:
time: 121 us
  Pallas kernels  120 us (99%)
  local copies, waits for them, and re-layouts  1.38 us (1%)
    pallas_call x1, Pallas kernels, body(): pl.pallas_call(kernel, out_shape=jax.ShapeDtypeStruct((T, T), BF16), in_s...  120 us

profile of v7, /device:TPU:1, one launch (start us, length us, event | category | flops | bytes accessed | tf_op | source)
XLA Modules:
  0.0 121.1 jit_solution(4440975146520272428)
XLA Ops:
  0.0 119.7 %relay.1 = bf16[128,128]{1,0:T(8,128)(2,1)} custom-call(bf16[4096,2,256]{2,1,0:T(2,128)(2,1)} %bitcast.12, bf16[2,32,4096]{2,1,0:T(8,128)(2,1)} %bitcast.14, bf16[256,4096]{1,0:T(8,128)(2,1)} %bitcast.13, f32[1,4]{1,0:T(1,128)} %bias_hbm.1, f32[1,4]{1,0:T(1,128)} %decay_hbm.1, f32[1,4]{1,0:T(1,128)} %skip_hbm.1, bf16[4,4096]{1,0:T(4,128)(2,1)} %bitcast.18, ...), custom_call_target="tpu_custom_call" | custom-call | tf_op jit(solution)/shard_map/relay/pallas_call | solution.py:527
  119.7 1.4 %copy.16 = bf16[1,128,128]{2,1,0:T(8,128)(2,1)} copy(bf16[1,128,128]{2,1,0:T(8,128)(2,1)} %bitcast.17) | data formatting | bytes 65536
